TPU v7x, 256 devices: a whole 4x4x8 slice. The times are simulated.
256 devices in a mesh: gx: 16 (over y, x), gy: 16 (over z, core).
Axes of the slice: x: 4, y: 4, z: 8, core: 2. Of those that a mesh axis runs over, the one named last changes fastest.
Arguments:
- volume: float32 [512, 1024, 256], P('gx', 'gy'), may hold values from -18 to 18, as said below
Outputs:
- denoised: float32 [512, 1024, 256], P('gx', 'gy')
Inputs may be any that keep to these rules, and one draw needn't show every extreme that they name: `volume`: real values.
All inputs are finite; a program needn't handle non-finite values.
Results may differ from a plain program's by a relative error of at most 0.00002.
Values sent between devices are 32-bit elements; how exact they have to be, the bound alone decides.
No kernel may reach another device: no remote copies, remote signals or barrier semaphores. Data moves between devices by JAX's collectives and lax.ppermute only.
A program may use at most 128 MiB of HBM per device.

v0:
```python
import math

import jax
import jax.numpy as jnp
import numpy as np
from jax import lax
from jax.experimental import pallas as pl
from jax.experimental.pallas import tpu as pltpu
from jax.sharding import PartitionSpec as P

R3 = math.sqrt(3.0)
NEAR = R3 / 4.0
FAR = (R3 - 2.0) / 4.0
K0 = (R3 - 1.0) / math.sqrt(2.0)
K1 = (R3 + 1.0) / math.sqrt(2.0)
DD, SS = K1 * K1, K0 * K0
F32 = jnp.float32
BF16 = jnp.bfloat16
VMEM = pl.BlockSpec(memory_space=pltpu.VMEM)


def depth_matrix(n):
    v = np.eye(n)
    e, o = v[:, 0::2], v[:, 1::2]
    s = e + R3 * o
    d = o - NEAR * s - FAR * np.roll(s, 1, axis=1)
    s = s - np.roll(d, -1, axis=1)
    return np.concatenate([K0 * s, K1 * d], axis=1)


def halves(m):
    m = np.asarray(m, np.float32)
    hi = m.astype(BF16)
    lo = (m - hi.astype(np.float32)).astype(BF16)
    return jnp.asarray(hi), jnp.asarray(lo)


def times(x, hi_ref, lo_ref):
    hi = x.astype(BF16)
    lo = (x - hi.astype(F32)).astype(BF16)
    w, v = hi_ref[...], lo_ref[...]
    dot = lambda p, q: jnp.dot(p, q, preferred_element_type=F32)
    return dot(hi, w) + (dot(lo, w) + dot(hi, v))


def lift_x(load, store, pairs):
    o = load(1)
    s0 = load(0) + R3 * o
    o = load(3)
    s1 = load(2) + R3 * o
    d1 = o - NEAR * s1 - FAR * s0
    for m in range(1, pairs - 1):
        o = load(2 * m + 3)
        s2 = load(2 * m + 2) + R3 * o
        d2 = o - NEAR * s2 - FAR * s1
        store(m - 1, 0, d1)
        store(m - 1, 1, s1 - d2)
        s1, d1 = s2, d2


def lift_y(load):
    s0 = load(0) + R3 * load(1)
    o1 = load(3)
    s1 = load(2) + R3 * o1
    o2 = load(5)
    s2 = load(4) + R3 * o2
    d1 = o1 - NEAR * s1 - FAR * s0
    d2 = o2 - NEAR * s2 - FAR * s1
    return d1, s1 - d2


def unlift(d0, d1, sm, s0):
    first = s0 + d1
    o = d0 + NEAR * first + FAR * (sm + d0)
    return first - R3 * o, o


def unlift_x(load, store, pairs):
    d1 = load(1, 0)
    before = load(0, 1) + d1
    for m in range(1, pairs - 1):
        d2 = load(m + 1, 0)
        first = load(m, 1) + d2
        o = d1 + NEAR * first + FAR * before
        store(2 * m - 2, first - R3 * o)
        store(2 * m - 1, o)
        d1, before = d2, first


def shrink(c, t):
    return c - jnp.clip(c, -t, t)


def forward_one(vol, hx, hy, wh, wl, c1, cc1, m2x, ex, ey, ext, zin):
    @pl.loop(0, 4)
    def _(c):
        rows = pl.ds(pl.multiple_of(c * 16, 16), 16)

        def load(k):
            return vol[k, rows, :] if k < 32 else hx[k - 32, rows, :]

        def store(i, p, v):
            ext[i, p, 0, rows, :] = v[:, :128]
            ext[i, p, 1, rows, :] = v[:, 128:]

        lift_x(load, store, 18)

    def put(i, p, v):
        ext[i, p, 0, 64:68, :] = v[:, :128]
        ext[i, p, 1, 64:68, :] = v[:, 128:]

    lift_x(lambda k: hy[k], put, 18)

    def group(g, acc):
        for q in range(4):
            for p in range(2):
                i = g * 4 + q
                base = (q * 2 + p) * 64
                for h in range(2):
                    d, s = lift_y(lambda k: ext[i, p, h, pl.ds(k, 32, stride=2), :])
                    lanes = slice(h * 128, h * 128 + 128)
                    zin[base : base + 32, lanes] = d
                    zin[base + 32 : base + 64, lanes] = s
        u = times(zin[...], wh, wl).reshape(4, 2, 2, 32, 256)
        c1[pl.ds(g * 4, 4)] = u
        cc1[pl.ds(g * 4, 4)] = u[:, 1, 1, :, :128]
        return acc + jnp.sum(jnp.abs(u[:, 0, 0, :, 128:]).reshape(16, 8, 128), axis=0)

    acc = lax.fori_loop(0, 4, group, jnp.zeros((8, 128), F32))
    m2x[0:13] = cc1[0:13]
    m2x[13] = jnp.full((32, 128), jnp.sum(acc), F32)
    ex[0] = c1[14, 1]
    ex[1] = c1[15, 0]
    ex[2] = c1[15, 1]
    for i in range(16):
        for p in range(2):
            ey[2 * i + p, 0:1, :] = c1[i, p, 1, 30:31, :]
            ey[2 * i + p, 1:2, :] = c1[i, p, 0, 31:32, :]
            ey[2 * i + p, 2:3, :] = c1[i, p, 1, 31:32, :]
            ey[2 * i + p, 3:4, :] = c1[i, p, 1, 31:32, :]


def pack_two(cc1, m2x, r2x, m2y):
    m2y[0:15] = cc1[1:16, 0:16]
    m2y[15:28] = r2x[0:13, 0:16]
    m2y[28] = m2x[13, 0:16] + r2x[13, 0:16]


def forward_rest(
    cc1, r2x, r2y, ex, w2h, w2l, w3h, w3l, c2, c3, m3x, x2, z2, x3, z3
):
    def near(k):
        return cc1[k + 1] if k < 15 else r2x[k - 15]

    def put_near(i, p, v):
        x2[i, p, 0:32, :] = v

    def put_far(i, p, v):
        x2[i, p, 32:48, :] = v
        x2[i, p, 48:56, :] = jnp.zeros((8, 128), F32)

    lift_x(near, put_near, 14)
    lift_x(lambda k: r2y[k], put_far, 14)
    for i in range(12):
        for p in range(2):
            d, s = lift_y(lambda k: x2[i, p, pl.ds(k + 1, 24, stride=2), :])
            base = (i * 2 + p) * 48
            z2[base : base + 24, :] = d
            z2[base + 24 : base + 48, :] = s
    c2[...] = times(z2[...], w2h, w2l).reshape(12, 2, 2, 24, 128)

    def put3(i, p, v):
        x3[i, p, :, :] = v

    lift_x(lambda k: c2[k, 1, 1], put3, 6)
    for i in range(4):
        for p in range(2):
            d, s = lift_y(lambda k: x3[i, p, pl.ds(k, 8, stride=2), :])
            base = (i * 2 + p) * 16
            z3[base : base + 8, :] = d
            z3[base + 8 : base + 16, :] = s
    u = times(z3[...], w3h, w3l)
    c3[...] = u.reshape(4, 2, 2, 8, 128)
    m3x[0:128, :] = u
    m3x[128:384, :] = c2[4:8, :, :, 0:16, :].reshape(256, 128)
    e = ex[...].reshape(192, 256)
    m3x[384:576, :] = e[:, :128]
    m3x[576:768, :] = e[:, 128:]


def left_one(r3x, k):
    lo = r3x[384 + 64 * k : 448 + 64 * k, :]
    hi = r3x[576 + 64 * k : 640 + 64 * k, :]
    return jnp.concatenate([lo, hi], axis=1).reshape(2, 32, 256)


def pack_three(c2, c3, ey, r3x, m3y):
    for i in range(8):
        for p in range(2):
            for q in range(2):
                at = ((i * 2 + p) * 2 + q) * 4
                if i < 4:
                    src = ((i * 2 + p) * 2 + q) * 8 + 4
                    m3y[at : at + 4, :] = r3x[src : src + 4, :]
                else:
                    m3y[at : at + 4, :] = c3[i - 4, p, q, 4:8, :]
    for i in range(12):
        for p in range(2):
            for q in range(2):
                at = 128 + ((i * 2 + p) * 2 + q) * 4
                if i < 4:
                    src = 128 + ((i * 2 + p) * 2 + q) * 16 + 12
                    m3y[at : at + 4, :] = r3x[src : src + 4, :]
                else:
                    m3y[at : at + 4, :] = c2[i - 4, p, q, 12:16, :]
    for k in range(34):
        at = 320 + k * 4
        if k < 3:
            for h in range(2):
                src = 384 + 192 * h + 64 * k
                to = at + 136 * h
                m3y[to : to + 1, :] = r3x[src + 62 : src + 63, :]
                m3y[to + 1 : to + 2, :] = r3x[src + 31 : src + 32, :]
                m3y[to + 2 : to + 3, :] = r3x[src + 63 : src + 64, :]
                m3y[to + 3 : to + 4, :] = r3x[src + 63 : src + 64, :]
        else:
            m3y[at : at + 4, :] = ey[k - 3, :, 0:128]
            m3y[at + 136 : at + 140, :] = ey[k - 3, :, 128:256]


def inverse_all(
    c1, c2, c3, r3x, r3y, ta, tb, w1h, w1l, w2h, w2l, w3h, w3l, out,
    u3, y3, z3, u2, y2, z2, dd, ss, y1, z1, *, factor
):
    noise = (ta[0:1, :] + tb[0:1, :]) * factor
    wide = jnp.concatenate([noise, noise], axis=1)
    scale = {(0, 0): 1.0 / DD, (0, 1): 1.0, (1, 0): 1.0, (1, 1): DD}

    for i in range(8):
        for p in range(2):
            for q in range(2):
                t = noise * (scale[p, q] * DD * DD)
                n = (i * 2 + p) * 2 + q
                if i < 4:
                    mid = r3x[n * 8 : n * 8 + 8, :]
                else:
                    mid = c3[i - 4, p, q]
                top = r3y[n * 4 : n * 4 + 4, :]
                u3[i, p, q, 4:8, :] = shrink(top, t)
                if p and q:
                    low = lax.broadcasted_iota(jnp.int32, (8, 128), 1) < 32
                    u3[i, p, q, 8:16, :] = jnp.where(low, mid, shrink(mid, t))
                    low = low[0:4]
                    u3[i, p, q, 4:8, :] = jnp.where(low, top, shrink(top, t))
                else:
                    u3[i, p, q, 8:16, :] = shrink(mid, t)
            e, o = unlift(
                u3[i, p, 0, 5:15, :],
                u3[i, p, 0, 6:16, :],
                u3[i, p, 1, 4:14, :],
                u3[i, p, 1, 5:15, :],
            )
            y3[i, p, 0:4, :] = jnp.zeros((4, 128), F32)
            y3[i, p, pl.ds(4, 10, stride=2), :] = e
            y3[i, p, pl.ds(5, 10, stride=2), :] = o

    def put3(k, v):
        z3[k * 24 : k * 24 + 24, :] = v

    unlift_x(lambda m, p: y3[m, p], put3, 8)
    rb2 = times(z3[...], w3h, w3l).reshape(12, 24, 128)

    for i in range(12):
        for p in range(2):
            for q in range(2):
                t = noise * (scale[p, q] * DD)
                n = (i * 2 + p) * 2 + q
                if i < 4:
                    mid = r3x[128 + n * 16 : 144 + n * 16, :]
                else:
                    mid = c2[i - 4, p, q, 0:16, :]
                u2[i, p, q, 4:8, :] = shrink(r3y[128 + n * 4 : 132 + n * 4, :], t)
                u2[i, p, q, 8:24, :] = shrink(mid, t)
            if p:
                u2[i, 1, 1, :, 0:64] = rb2[i][:, 0:64]
            e, o = unlift(
                u2[i, p, 0, 5:23, :],
                u2[i, p, 0, 6:24, :],
                u2[i, p, 1, 4:22, :],
                u2[i, p, 1, 5:23, :],
            )
            y2[i, p, 0:8, :] = jnp.zeros((8, 128), F32)
            y2[i, p, 40:48, :] = jnp.zeros((8, 128), F32)
            y2[i, p, pl.ds(5, 18, stride=2), :] = e
            y2[i, p, pl.ds(6, 18, stride=2), :] = o

    def put2(k, v):
        z2[k * 48 : k * 48 + 48, :] = v

    unlift_x(lambda m, p: y2[m, p], put2, 12)
    z2[...] = times(z2[...], w2h, w2l)

    t_d = {p: wide * scale[p, 0] for p in range(2)}
    t_s = {p: wide * scale[p, 1] for p in range(2)}

    def layer(l, p, mid_d, mid_s, cell):
        lo, hi = r3y[pl.ds(320 + l * 4, 4), :], r3y[pl.ds(456 + l * 4, 4), :]
        top = jnp.concatenate([lo, hi], axis=1)
        dd[p, 7:8, :] = shrink(top[1:2], t_d[p])
        dd[p, 8:40, :] = shrink(mid_d, t_d[p])
        ss[p, 6:7, :] = shrink(top[0:1], t_s[p])
        ss[p, 7:8, :] = shrink(top[2:3], t_s[p])
        ss[p, 8:40, :] = shrink(mid_s, t_s[p])
        if p:
            ss[p, :, 0:128] = z2[pl.ds(cell * 48, 40), :]
        e, o = unlift(
            dd[p, 7:39, :], dd[p, 8:40, :], ss[p, 6:38, :], ss[p, 7:39, :]
        )
        for h in range(2):
            y1[l, h, pl.ds(0, 32, stride=2), :] = e[:, h * 128 : h * 128 + 128]
            y1[l, h, pl.ds(1, 32, stride=2), :] = o[:, h * 128 : h * 128 + 128]

    for k in range(3):
        mid = left_one(r3x, k)
        layer(k, 1 - k % 2, mid[0], mid[1], (k - 2) // 2 + 2)

    @pl.loop(0, 15)
    def _(i):
        layer(2 * i + 3, 0, c1[i, 0, 0], c1[i, 0, 1], None)
        layer(2 * i + 4, 1, c1[i, 1, 0], c1[i, 1, 1], i + 3)

    layer(33, 0, c1[15, 0, 0], c1[15, 0, 1], None)

    @pl.loop(0, 4)
    def _(c):
        rows = pl.ds(pl.multiple_of(c * 16, 16), 16)

        for h in range(2):

            def load(m, p):
                return y1[2 * m - 1 + p, h, rows, :]

            def put(k, v):
                z1[k, rows, h * 128 : h * 128 + 128] = v

            unlift_x(load, put, 18)

    @pl.loop(0, 4)
    def _(g):
        u = times(z1[pl.ds(g * 8, 8)].reshape(512, 256), w1h, w1l)
        out[pl.ds(g * 8, 8)] = u.reshape(8, 64, 256)


def call(body, outs, scratch, args, vmem_mib):
    return pl.pallas_call(
        body,
        out_shape=[jax.ShapeDtypeStruct(s, F32) for s in outs],
        in_specs=[VMEM] * len(args),
        out_specs=[VMEM] * len(outs),
        scratch_shapes=[pltpu.VMEM(s, F32) for s in scratch],
        compiler_params=pltpu.CompilerParams(vmem_limit_bytes=vmem_mib << 20),
    )(*args)


def from_ahead(v, axis, by):
    n = lax.axis_size(axis)
    return lax.ppermute(v, axis, [((i + by) % n, i) for i in range(n)])


def from_behind(v, axis):
    n = lax.axis_size(axis)
    return lax.ppermute(v, axis, [(i, (i + 1) % n) for i in range(n)])


def on_device(volume):
    w = {n: depth_matrix(n) for n in (256, 128, 64)}
    w[64] = np.pad(w[64], ((0, 64), (0, 64)))
    f1, f2, f3 = halves(w[256]), halves(w[128]), halves(w[64])
    b1, b2, b3 = halves(w[256].T), halves(w[128].T), halves(w[64].T)
    nx, ny = lax.axis_size("gx"), lax.axis_size("gy")

    hx = from_ahead(volume[0:4], "gx", 1)
    hy = from_ahead(
        jnp.concatenate([volume[:, 0:4], hx[:, 0:4]], axis=0), "gy", 1
    )
    c1, cc1, m2x, ex, ey = call(
        forward_one,
        [(16, 2, 2, 32, 256), (16, 32, 128), (14, 32, 128), (3, 2, 32, 256), (32, 4, 256)],
        [(16, 2, 2, 72, 128), (512, 256)],
        [volume, hx, hy, *f1],
        24,
    )
    r2x = from_ahead(m2x, "gx", 1)
    (m2y,) = call(pack_two, [(29, 16, 128)], [], [cc1, m2x, r2x], 8)
    r2y = from_ahead(m2y, "gy", 1)
    total = m2y[28, 0:8] + r2y[28, 0:8]
    steps = [(a, 1 << k) for a, n in (("gx", nx), ("gy", ny)) for k in range(1, 8) if 1 << k < n]
    other = jnp.zeros_like(total)
    for k, (axis, by) in enumerate(steps):
        other = from_ahead(total, axis, by)
        if k < len(steps) - 1:
            total = total + other

    c2, c3, m3x = call(
        forward_rest,
        [(12, 2, 2, 24, 128), (4, 2, 2, 8, 128), (768, 128)],
        [(12, 2, 56, 128), (1152, 128), (4, 2, 24, 128), (128, 128)],
        [cc1, r2x, r2y, ex, *f2, *f3],
        12,
    )
    r3x = from_behind(m3x, "gx")
    (m3y,) = call(pack_three, [(592, 128)], [], [c2, c3, ey, r3x], 8)
    r3y = from_behind(m3y, "gy")
    count = nx * ny * volume.size // 8
    factor = math.sqrt(math.pi / 2.0) / count * DD

    def body(*refs):
        inverse_all(*refs, factor=factor)

    (out,) = call(
        body,
        [volume.shape],
        [
            (8, 2, 2, 16, 128), (8, 2, 24, 128), (288, 128),
            (12, 2, 2, 24, 128), (12, 2, 48, 128), (960, 128),
            (2, 40, 256), (2, 40, 256), (34, 2, 64, 128), (32, 64, 256),
        ],
        [c1, c2, c3, r3x, r3y, total, other, *b1, *b2, *b3],
        24,
    )
    return out


def solution(mesh):
    return jax.shard_map(
        on_device,
        mesh=mesh,
        in_specs=(P("gx", "gy", None),),
        out_specs=P("gx", "gy", None),
        check_vma=False,
    )
```

profile of v0, /device:TPU:30, one launch (start us, length us, event | category | flops | bytes accessed | tf_op | source)
XLA Modules:
  0.0 91.0 jit_solution(15902102973874684765)
XLA Ops:
  0.0 1.0 %slice.15 = f32[4,64,256]{2,1,0:T(8,128)S(1)} slice(f32[32,64,256]{2,1,0:T(8,128)} %vol.1), slice={[0:4], [0:64], [0:256]} | slice | bytes 524288 | tf_op jit(solution)/shard_map/slice | solution.py:382
  1.0 0.9 collective-permute-start
  1.9 1.0 %slice.16 = f32[32,4,256]{2,1,0:T(4,128)S(1)} slice(f32[32,64,256]{2,1,0:T(8,128)} %vol.1), slice={[0:32], [0:4], [0:256]} | slice | bytes 262144 | tf_op jit(solution)/shard_map/slice | solution.py:384
  2.9 9.6 %collective-permute-done.hx = f32[4,64,256]{2,1,0:T(8,128)S(1)} collective-permute-done((f32[4,64,256]{2,1,0:T(8,128)S(1)}, f32[4,64,256]{2,1,0:T(8,128)S(1)}, u32[]{:S(2)}, u32[]{:S(2)}) %collective-permute-start) | collective-permute-done | bytes 262176 | tf_op jit(solution)/shard_map/ppermute | solution.py:367
  12.5 4.5 %collective-permute-start.1 = (f32[36,4,256]{2,1,0:T(4,128)S(1)}, f32[36,4,256]{2,1,0:T(4,128)S(1)}, u32[]{:S(2)}, u32[]{:S(2)}) collective-permute-start(f32[36,4,256]{2,1,0:T(4,128)S(1)} %pad_maximum_fusion), channel_id=1, source_target_pairs={{1,0},{2,1},{3,2},{4,3},{5,4},{6,5},{7,6},{8,7},{9,8},{10,9},{11,1... | collective-permute-start | bytes 442376 | tf_op jit(solution)/shard_map/ppermute | solution.py:367
  17.0 2.7 %collective-permute-done.1.hy = f32[36,4,256]{2,1,0:T(4,128)S(1)} collective-permute-done((f32[36,4,256]{2,1,0:T(4,128)S(1)}, f32[36,4,256]{2,1,0:T(4,128)S(1)}, u32[]{:S(2)}, u32[]{:S(2)}) %collective-permute-start.1) | collective-permute-done | bytes 147488 | tf_op jit(solution)/shard_map/ppermute | solution.py:367
  19.6 1.6 %copy-done = f32[32,64,256]{2,1,0:T(8,128)S(1)} copy-done((f32[32,64,256]{2,1,0:T(8,128)S(1)}, f32[32,64,256]{2,1,0:T(8,128)}, u32[]{:S(2)}) %copy-start) | copy-done | bytes 2097176
  21.2 0.9 copy-done.3
  22.1 0.9 copy-done.4
  23.0 2.1 %shard_map.127 = (f32[16,2,2,32,256]{4,3,2,1,0:T(8,128)S(1)}, f32[16,32,128]{2,1,0:T(8,128)S(1)}, f32[14,32,128]{2,1,0:T(8,128)S(1)}, f32[3,2,32,256]{3,2,1,0:T(8,128)S(1)}, f32[32,4,256]{2,1,0:T(4,128)S(1)}) custom-call(f32[32,64,256]{2,1,0:T(8,128)S(1)} %copy-done, f32[4,64,256]{2,1,0:T(8,128)S(1)} %collective-permute-done.hx, ...), custom_call_target="tpu_custom_call" | custom-call | tf_op jit(solution)/shard_map/pallas_call | solution.py:355
  25.3 9.3 %collective-permute-done.2.r2x = f32[14,32,128]{2,1,0:T(8,128)S(1)} collective-permute-done((f32[14,32,128]{2,1,0:T(8,128)S(1)}, f32[14,32,128]{2,1,0:T(8,128)S(1)}, u32[]{:S(2)}, u32[]{:S(2)}) %collective-permute-start.2) | collective-permute-done | bytes 229408 | tf_op jit(solution)/shard_map/ppermute | solution.py:367
  34.6 3.3 %collective-permute-start.3 = (f32[29,16,128]{2,1,0:T(8,128)S(1)}, f32[29,16,128]{2,1,0:T(8,128)S(1)}, u32[]{:S(2)}, u32[]{:S(2)}) collective-permute-start(f32[29,16,128]{2,1,0:T(8,128)S(1)} %shard_map.128), channel_id=1, source_target_pairs={{1,0},{2,1},{3,2},{4,3},{5,4},{6,5},{7,6},{8,7},{9,8},{10,9},{11,1... | collective-permute-start | bytes 712712 | tf_op jit(solution)/shard_map/ppermute | solution.py:367
  38.0 3.6 %collective-permute-done.3.r2y = f32[29,16,128]{2,1,0:T(8,128)S(1)} collective-permute-done((f32[29,16,128]{2,1,0:T(8,128)S(1)}, f32[29,16,128]{2,1,0:T(8,128)S(1)}, u32[]{:S(2)}, u32[]{:S(2)}) %collective-permute-start.3) | collective-permute-done | bytes 237600 | tf_op jit(solution)/shard_map/ppermute | solution.py:367
  42.5 7.8 %collective-permute-done.4.r3x.refs_3_ = f32[768,128]{1,0:T(8,128)S(1)} collective-permute-done((f32[768,128]{1,0:T(8,128)S(1)}, f32[768,128]{1,0:T(8,128)S(1)}, u32[]{:S(2)}, u32[]{:S(2)}) %collective-permute-start.4) | collective-permute-done | bytes 393248 | tf_op jit(solution)/shard_map/ppermute | solution.py:372
  50.5 7.2 %collective-permute-done.6 = f32[8,128]{1,0:T(8,128)S(1)} collective-permute-done((f32[8,128]{1,0:T(8,128)S(1)}, f32[8,128]{1,0:T(8,128)S(1)}, u32[]{:S(2)}, u32[]{:S(2)}) %collective-permute-start.6) | collective-permute-done | bytes 4128 | tf_op jit(solution)/shard_map/ppermute | solution.py:367
  57.7 4.8 %collective-permute-done.7 = f32[8,128]{1,0:T(8,128)S(1)} collective-permute-done((f32[8,128]{1,0:T(8,128)S(1)}, f32[8,128]{1,0:T(8,128)S(1)}, u32[]{:S(2)}, u32[]{:S(2)}) %collective-permute-start.7) | collective-permute-done | bytes 4128 | tf_op jit(solution)/shard_map/ppermute | solution.py:367
  62.6 5.1 %collective-permute-done.8 = f32[8,128]{1,0:T(8,128)S(1)} collective-permute-done((f32[8,128]{1,0:T(8,128)S(1)}, f32[8,128]{1,0:T(8,128)S(1)}, u32[]{:S(2)}, u32[]{:S(2)}) %collective-permute-start.8) | collective-permute-done | bytes 4128 | tf_op jit(solution)/shard_map/ppermute | solution.py:367
  67.7 4.9 %collective-permute-start.9 = (f32[8,128]{1,0:T(8,128)S(1)}, f32[8,128]{1,0:T(8,128)S(1)}, u32[]{:S(2)}, u32[]{:S(2)}) collective-permute-start(f32[8,128]{1,0:T(8,128)S(1)} %add.25), channel_id=1, source_target_pairs={{2,0},{3,1},{4,2},{5,3},{6,4},{7,5},{8,6},{9,7},{10,8},{11,9},{12,... | collective-permute-start | bytes 12296 | tf_op jit(solution)/shard_map/ppermute | solution.py:367
  72.6 1.3 %collective-permute-done.9 = f32[8,128]{1,0:T(8,128)S(1)} collective-permute-done((f32[8,128]{1,0:T(8,128)S(1)}, f32[8,128]{1,0:T(8,128)S(1)}, u32[]{:S(2)}, u32[]{:S(2)}) %collective-permute-start.9) | collective-permute-done | bytes 4128 | tf_op jit(solution)/shard_map/ppermute | solution.py:367
  73.9 2.7 %collective-permute-start.10 = (f32[8,128]{1,0:T(8,128)S(1)}, f32[8,128]{1,0:T(8,128)S(1)}, u32[]{:S(2)}, u32[]{:S(2)}) collective-permute-start(f32[8,128]{1,0:T(8,128)S(1)} %add.26), channel_id=1, source_target_pairs={{4,0},{5,1},{6,2},{7,3},{8,4},{9,5},{10,6},{11,7},{12,8},{13,9},{1... | collective-permute-start | bytes 12296 | tf_op jit(solution)/shard_map/ppermute | solution.py:367
  76.6 1.8 %collective-permute-done.10 = f32[8,128]{1,0:T(8,128)S(1)} collective-permute-done((f32[8,128]{1,0:T(8,128)S(1)}, f32[8,128]{1,0:T(8,128)S(1)}, u32[]{:S(2)}, u32[]{:S(2)}) %collective-permute-start.10) | collective-permute-done | bytes 4128 | tf_op jit(solution)/shard_map/ppermute | solution.py:367
  78.4 2.9 %collective-permute-start.11 = (f32[8,128]{1,0:T(8,128)S(1)}, f32[8,128]{1,0:T(8,128)S(1)}, u32[]{:S(2)}, u32[]{:S(2)}) collective-permute-start(f32[8,128]{1,0:T(8,128)S(1)} %add.27.refs_5_), channel_id=1, source_target_pairs={{8,0},{9,1},{10,2},{11,3},{12,4},{13,5},{14,6},{15,7},{0,8},{1,9},... | collective-permute-start | bytes 12296 | tf_op jit(solution)/shard_map/ppermute | solution.py:367
  81.3 4.7 %collective-permute-done.11.refs_6_ = f32[8,128]{1,0:T(8,128)S(1)} collective-permute-done((f32[8,128]{1,0:T(8,128)S(1)}, f32[8,128]{1,0:T(8,128)S(1)}, u32[]{:S(2)}, u32[]{:S(2)}) %collective-permute-start.11) | collective-permute-done | bytes 4128 | tf_op jit(solution)/shard_map/ppermute | solution.py:367
  86.0 5.1 %shard_map.131 = f32[32,64,256]{2,1,0:T(8,128)} custom-call(f32[16,2,2,32,256]{4,3,2,1,0:T(8,128)S(1)} %get-tuple-element.13.refs_0_, f32[12,2,2,24,128]{4,3,2,1,0:T(8,128)S(1)} %get-tuple-element.17.c2.refs_1_, f32[4,2,2,8,128]{4,3,2,1,0:T(8,128)S(1)} %get-tuple-element.18.c3.refs_2_, f32[768,128]{1,0:T(8,128)S(1)} %collective-permute-done.4.r3x.refs_3_, ...), custom_call_target="tpu_custom_call" | custom-call | tf_op jit(solution)/shard_map/pallas_call | solution.py:355
  (41 shorter events, 1.3 us)
Async XLA Ops:
  1.0 40.6 %copy-start.9 = (bf16[128,128]{1,0:T(8,128)(2,1)S(1)}, bf16[128,128]{1,0:T(8,128)(2,1)}, u32[]{:S(2)}) copy-start(bf16[128,128]{1,0:T(8,128)(2,1)} %constant.29.clone.w3l) | copy-start | bytes 98308
  1.0 40.6 %copy-start.10 = (bf16[128,128]{1,0:T(8,128)(2,1)S(1)}, bf16[128,128]{1,0:T(8,128)(2,1)}, u32[]{:S(2)}) copy-start(bf16[128,128]{1,0:T(8,128)(2,1)} %constant.28.clone.w3h) | copy-start | bytes 98308
  1.0 40.6 %copy-start.11 = (bf16[128,128]{1,0:T(8,128)(2,1)S(1)}, bf16[128,128]{1,0:T(8,128)(2,1)}, u32[]{:S(2)}) copy-start(bf16[128,128]{1,0:T(8,128)(2,1)} %constant.27.clone.w2l) | copy-start | bytes 98308
  1.0 40.6 %copy-start.12 = (bf16[128,128]{1,0:T(8,128)(2,1)S(1)}, bf16[128,128]{1,0:T(8,128)(2,1)}, u32[]{:S(2)}) copy-start(bf16[128,128]{1,0:T(8,128)(2,1)} %constant.26.clone.w2h) | copy-start | bytes 98308
  1.0 11.4 %collective-permute-start = (f32[4,64,256]{2,1,0:T(8,128)S(1)}, f32[4,64,256]{2,1,0:T(8,128)S(1)}, u32[]{:S(2)}, u32[]{:S(2)}) collective-permute-start(f32[4,64,256]{2,1,0:T(8,128)S(1)} %slice.15), channel_id=1, source_target_pairs={{16,0},{32,16},{48,32},{64,48},{80,64},{96,80},{112,96},{128,112},... | collective-permute-start | bytes 786440 | tf_op jit(solution)/shard_map/ppermute | solution.py:367
  12.5 7.1 %collective-permute-start.1 = (f32[36,4,256]{2,1,0:T(4,128)S(1)}, f32[36,4,256]{2,1,0:T(4,128)S(1)}, u32[]{:S(2)}, u32[]{:S(2)}) collective-permute-start(f32[36,4,256]{2,1,0:T(4,128)S(1)} %pad_maximum_fusion), channel_id=1, source_target_pairs={{1,0},{2,1},{3,2},{4,3},{5,4},{6,5},{7,6},{8,7},{9,8},{10,9},{11,1... | collective-permute-start | bytes 442376 | tf_op jit(solution)/shard_map/ppermute | solution.py:367
  19.6 1.6 %copy-start = (f32[32,64,256]{2,1,0:T(8,128)S(1)}, f32[32,64,256]{2,1,0:T(8,128)}, u32[]{:S(2)}) copy-start(f32[32,64,256]{2,1,0:T(8,128)} %vol.1) | copy-start | bytes 6291460
  21.2 0.9 copy-start.3
  25.1 60.8 %copy-start.1 = (bf16[256,256]{1,0:T(8,128)(2,1)S(1)}, bf16[256,256]{1,0:T(8,128)(2,1)}, u32[]{:S(2)}) copy-start(bf16[256,256]{1,0:T(8,128)(2,1)} %constant.31.clone.refs_8_) | copy-start | bytes 393220
  25.1 60.8 %copy-start.2 = (bf16[256,256]{1,0:T(8,128)(2,1)S(1)}, bf16[256,256]{1,0:T(8,128)(2,1)}, u32[]{:S(2)}) copy-start(bf16[256,256]{1,0:T(8,128)(2,1)} %constant.30.clone.refs_7_) | copy-start | bytes 393220
  25.1 60.8 %copy-start.5 = (bf16[128,128]{1,0:T(8,128)(2,1)S(1)}, bf16[128,128]{1,0:T(8,128)(2,1)}, u32[]{:S(2)}) copy-start(bf16[128,128]{1,0:T(8,128)(2,1)} %constant.35.clone.refs_12_) | copy-start | bytes 98308
  25.2 60.8 %copy-start.6 = (bf16[128,128]{1,0:T(8,128)(2,1)S(1)}, bf16[128,128]{1,0:T(8,128)(2,1)}, u32[]{:S(2)}) copy-start(bf16[128,128]{1,0:T(8,128)(2,1)} %constant.34.clone.refs_11_) | copy-start | bytes 98308
  25.2 60.8 %copy-start.7 = (bf16[128,128]{1,0:T(8,128)(2,1)S(1)}, bf16[128,128]{1,0:T(8,128)(2,1)}, u32[]{:S(2)}) copy-start(bf16[128,128]{1,0:T(8,128)(2,1)} %constant.33.clone.refs_10_) | copy-start | bytes 98308
  25.2 60.8 %copy-start.8 = (bf16[128,128]{1,0:T(8,128)(2,1)S(1)}, bf16[128,128]{1,0:T(8,128)(2,1)}, u32[]{:S(2)}) copy-start(bf16[128,128]{1,0:T(8,128)(2,1)} %constant.32.clone.refs_9_) | copy-start | bytes 98308
  25.2 9.4 %collective-permute-start.2 = (f32[14,32,128]{2,1,0:T(8,128)S(1)}, f32[14,32,128]{2,1,0:T(8,128)S(1)}, u32[]{:S(2)}, u32[]{:S(2)}) collective-permute-start(f32[14,32,128]{2,1,0:T(8,128)S(1)} %get-tuple-element.15.m2x), channel_id=1, source_target_pairs={{16,0},{32,16},{48,32},{64,48},{80,64},{96,80},{112,96},{128,112},... | collective-permute-start | bytes 688136 | tf_op jit(solution)/shard_map/ppermute | solution.py:367
  34.6 6.9 %collective-permute-start.3 = (f32[29,16,128]{2,1,0:T(8,128)S(1)}, f32[29,16,128]{2,1,0:T(8,128)S(1)}, u32[]{:S(2)}, u32[]{:S(2)}) collective-permute-start(f32[29,16,128]{2,1,0:T(8,128)S(1)} %shard_map.128), channel_id=1, source_target_pairs={{1,0},{2,1},{3,2},{4,3},{5,4},{6,5},{7,6},{8,7},{9,8},{10,9},{11,1... | collective-permute-start | bytes 712712 | tf_op jit(solution)/shard_map/ppermute | solution.py:367
  42.4 7.9 %collective-permute-start.4 = (f32[768,128]{1,0:T(8,128)S(1)}, f32[768,128]{1,0:T(8,128)S(1)}, u32[]{:S(2)}, u32[]{:S(2)}) collective-permute-start(f32[768,128]{1,0:T(8,128)S(1)} %get-tuple-element.19), channel_id=1, source_target_pairs={{0,16},{16,32},{32,48},{48,64},{64,80},{80,96},{96,112},{112,128},... | collective-permute-start | bytes 1179656 | tf_op jit(solution)/shard_map/ppermute | solution.py:372
  50.4 35.5 %collective-permute-start.5 = (f32[592,128]{1,0:T(8,128)S(1)}, f32[592,128]{1,0:T(8,128)S(1)}, u32[]{:S(2)}, u32[]{:S(2)}) collective-permute-start(f32[592,128]{1,0:T(8,128)S(1)} %shard_map.130), channel_id=1, source_target_pairs={{0,1},{1,2},{2,3},{3,4},{4,5},{5,6},{6,7},{7,8},{8,9},{9,10},{10,1... | collective-permute-start | bytes 909320 | tf_op jit(solution)/shard_map/ppermute | solution.py:372
  50.4 7.3 %collective-permute-start.6 = (f32[8,128]{1,0:T(8,128)S(1)}, f32[8,128]{1,0:T(8,128)S(1)}, u32[]{:S(2)}, u32[]{:S(2)}) collective-permute-start(f32[8,128]{1,0:T(8,128)S(1)} %fusion), channel_id=1, source_target_pairs={{32,0},{48,16},{64,32},{80,48},{96,64},{112,80},{128,96},{144,112}... | collective-permute-start | bytes 12296 | tf_op jit(solution)/shard_map/ppermute | solution.py:367
  57.7 4.8 %collective-permute-start.7 = (f32[8,128]{1,0:T(8,128)S(1)}, f32[8,128]{1,0:T(8,128)S(1)}, u32[]{:S(2)}, u32[]{:S(2)}) collective-permute-start(f32[8,128]{1,0:T(8,128)S(1)} %add.23), channel_id=1, source_target_pairs={{64,0},{80,16},{96,32},{112,48},{128,64},{144,80},{160,96},{176,11... | collective-permute-start | bytes 12296 | tf_op jit(solution)/shard_map/ppermute | solution.py:367
  62.6 5.1 %collective-permute-start.8 = (f32[8,128]{1,0:T(8,128)S(1)}, f32[8,128]{1,0:T(8,128)S(1)}, u32[]{:S(2)}, u32[]{:S(2)}) collective-permute-start(f32[8,128]{1,0:T(8,128)S(1)} %add.24), channel_id=1, source_target_pairs={{128,0},{144,16},{160,32},{176,48},{192,64},{208,80},{224,96},{240... | collective-permute-start | bytes 12296 | tf_op jit(solution)/shard_map/ppermute | solution.py:367
  67.7 6.2 %collective-permute-start.9 = (f32[8,128]{1,0:T(8,128)S(1)}, f32[8,128]{1,0:T(8,128)S(1)}, u32[]{:S(2)}, u32[]{:S(2)}) collective-permute-start(f32[8,128]{1,0:T(8,128)S(1)} %add.25), channel_id=1, source_target_pairs={{2,0},{3,1},{4,2},{5,3},{6,4},{7,5},{8,6},{9,7},{10,8},{11,9},{12,... | collective-permute-start | bytes 12296 | tf_op jit(solution)/shard_map/ppermute | solution.py:367
  73.9 4.5 %collective-permute-start.10 = (f32[8,128]{1,0:T(8,128)S(1)}, f32[8,128]{1,0:T(8,128)S(1)}, u32[]{:S(2)}, u32[]{:S(2)}) collective-permute-start(f32[8,128]{1,0:T(8,128)S(1)} %add.26), channel_id=1, source_target_pairs={{4,0},{5,1},{6,2},{7,3},{8,4},{9,5},{10,6},{11,7},{12,8},{13,9},{1... | collective-permute-start | bytes 12296 | tf_op jit(solution)/shard_map/ppermute | solution.py:367
  78.4 7.5 %collective-permute-start.11 = (f32[8,128]{1,0:T(8,128)S(1)}, f32[8,128]{1,0:T(8,128)S(1)}, u32[]{:S(2)}, u32[]{:S(2)}) collective-permute-start(f32[8,128]{1,0:T(8,128)S(1)} %add.27.refs_5_), channel_id=1, source_target_pairs={{8,0},{9,1},{10,2},{11,3},{12,4},{13,5},{14,6},{15,7},{0,8},{1,9},... | collective-permute-start | bytes 12296 | tf_op jit(solution)/shard_map/ppermute | solution.py:367
  (1 other events, 0.9 us)
where the time goes:
time: 91.2 us; the launch traced here: 91 us
  waiting for transfers between devices  57.9 us (63%)
  starting transfers between devices  19.4 us (21%)
  Pallas kernels  8.05 us (9%)
  local copies, waits for them, and re-layouts  5.4 us (6%)
    ppermute x10, waiting for transfers between devices, from_ahead(): return lax.ppermute(v, axis, [((i + by) % n, i) for i in range(n)])  50.1 us
    ppermute x10, starting transfers between devices, from_ahead(): return lax.ppermute(v, axis, [((i + by) % n, i) for i in range(n)])  19.3 us
    pallas_call x5, Pallas kernels, call(): pl.pallas_call(body, out_shape=[jax.ShapeDtypeStruct(s, F32) for s in out...  8.05 us
    ppermute x2, waiting for transfers between devices, from_behind(): return lax.ppermute(v, axis, [(i, (i + 1) % n) for i in range(n)])  7.81 us
    unnamed x26, local copies, waits for them, and re-layouts  3.47 us
  transfers between devices with their start and end apart: 12, of which 11 were waited for; matrix products, arithmetic and copies ran while one was open for 1% of the time, Pallas kernels for 0%

commit v1 on v0

v1 whole, which is shorter than its diff:
```python
import math

import jax
import jax.numpy as jnp
from jax import lax
from jax.experimental import pallas as pl
from jax.experimental.pallas import tpu as pltpu
from jax.sharding import PartitionSpec as P

R3 = math.sqrt(3.0)
NEAR = R3 / 4.0
FAR = (R3 - 2.0) / 4.0
K0 = (R3 - 1.0) / math.sqrt(2.0)
K1 = (R3 + 1.0) / math.sqrt(2.0)
DD = K1 * K1
F32 = jnp.float32
BF16 = jnp.bfloat16
VMEM = pl.BlockSpec(memory_space=pltpu.VMEM)
HBM = pl.BlockSpec(memory_space=pltpu.HBM)


def depth_weights(n, hi_ref, lo_ref):
    shape = hi_ref.shape
    cell = lax.broadcasted_iota(jnp.int32, shape, 0)
    place = lax.broadcasted_iota(jnp.int32, shape, 1)
    at = (cell - 2 * place) & (n - 1)
    low = {0: 1 + FAR, 1: R3 * (1 + FAR), 2: NEAR, 3: NEAR * R3 - 1}
    high = {0: -NEAR, 1: 1 - NEAR * R3, n - 2: -FAR, n - 1: -FAR * R3}
    w = jnp.zeros(shape, F32)
    for k, v in low.items():
        w = jnp.where((at == k) & (place < n // 2), K0 * v, w)
    for k, v in high.items():
        w = jnp.where((at == k) & (place >= n // 2), K1 * v, w)
    if shape[0] > n:
        w = jnp.where((cell < n) & (place < n), w, 0.0)
    hi = w.astype(BF16)
    hi_ref[...] = hi
    lo_ref[...] = (w - hi.astype(F32)).astype(BF16)


def times(x, hi_ref, lo_ref, back=False):
    hi = x.astype(BF16)
    lo = (x - hi.astype(F32)).astype(BF16)
    w, v = hi_ref[...], lo_ref[...]
    dims = (((1,), (1 if back else 0,)), ((), ()))
    dot = lambda p, q: lax.dot_general(p, q, dims, preferred_element_type=F32)
    return dot(hi, w) + (dot(lo, w) + dot(hi, v))


def raw(cell):
    def pair(m):
        o = cell(2 * m + 1)
        s = cell(2 * m) + R3 * o
        return s, o - NEAR * s

    return pair


def lift_x(pair, store, pairs):
    s0, _ = pair(0)
    s1, q1 = pair(1)
    d1 = q1 - FAR * s0
    for m in range(1, pairs - 1):
        s2, q2 = pair(m + 1)
        d2 = q2 - FAR * s1
        store(m - 1, 0, d1)
        store(m - 1, 1, s1 - d2)
        s1, d1 = s2, d2


def lift_y(load):
    s0 = load(0) + R3 * load(1)
    o1 = load(3)
    s1 = load(2) + R3 * o1
    o2 = load(5)
    s2 = load(4) + R3 * o2
    d1 = o1 - NEAR * s1 - FAR * s0
    d2 = o2 - NEAR * s2 - FAR * s1
    return d1, s1 - d2


def unlift(d0, d1, sm, s0):
    first = s0 + d1
    o = d0 + NEAR * first + FAR * (sm + d0)
    return first - R3 * o, o


def unlift_x(load, store, pairs):
    d1 = load(1, 0)
    before = load(0, 1) + d1
    for m in range(1, pairs - 1):
        d2 = load(m + 1, 0)
        first = load(m, 1) + d2
        o = d1 + NEAR * first + FAR * before
        store(2 * m - 2, first - R3 * o)
        store(2 * m - 1, o)
        d1, before = d2, first


def shrink(c, t):
    return c - jnp.clip(c, -t, t)


def depth_one(vol, zc, wh, wl):
    depth_weights(256, wh, wl)

    @pl.loop(0, 4)
    def _(g):
        u = times(vol[pl.ds(g * 8, 8)].reshape(512, 256), wh, wl)
        zc[pl.ds(g * 8, 8)] = u.reshape(8, 64, 256)


def forward_one(
    zc, hx, hy, hd, c1, cc1, ahead, behind, part, ey, ext, hxz, hyz, wh, wl
):
    depth_weights(256, wh, wl)
    for k in range(35):
        hyz[4 * k : 4 * k + 4, :] = hy[k] if k < 32 else hd[k - 32]
    hyz[140:144, :] = jnp.zeros((4, 256), F32)
    hxz[...] = times(hx[...].reshape(192, 256), wh, wl).reshape(3, 64, 256)
    hyz[...] = times(hyz[...], wh, wl)

    def spread(cell, edge):
        inner = raw(cell)

        def pair(m):
            if m < 16:
                return inner(m)
            return (edge(0), edge(1)) if m == 16 else (None, edge(2))

        return pair

    @pl.loop(0, 4)
    def _(c):
        rows = pl.ds(pl.multiple_of(c * 16, 16), 16)

        def store(i, p, v):
            ext[i, p, 0, rows, :] = v[:, :128]
            ext[i, p, 1, rows, :] = v[:, 128:]

        lift_x(spread(lambda k: zc[k, rows, :], lambda k: hxz[k, rows, :]), store, 18)

    def put(i, p, v):
        ext[i, p, 0, 64:68, :] = v[:, :128]
        ext[i, p, 1, 64:68, :] = v[:, 128:]

    def line(k):
        return hyz[4 * k : 4 * k + 4, :]

    lift_x(spread(line, lambda k: line(k + 32)), put, 18)

    def pair(i, acc):
        for p in range(2):
            for h in range(2):
                d, s = lift_y(lambda k: ext[i, p, h, pl.ds(k, 32, stride=2), :])
                lanes = slice(h * 128, h * 128 + 128)
                c1[i, p, 0, :, lanes] = d
                c1[i, p, 1, :, lanes] = s
                if (p, h) == (0, 1):
                    acc = acc + jnp.abs(d)
                if (p, h) == (1, 0):
                    cc1[i] = s
        return acc

    acc = lax.fori_loop(0, 16, pair, jnp.zeros((32, 128), F32))
    part[...] = jnp.full(part.shape, jnp.sum(acc), F32)
    ahead[...] = cc1[0:13]
    behind[0:480, :] = cc1[1:16].reshape(480, 128)
    for k, (i, p) in enumerate(((14, 1), (15, 0), (15, 1))):
        for q in range(2):
            for h in range(2):
                at = 480 + 192 * h + 64 * k + 32 * q
                behind[at : at + 32, :] = c1[i, p, q, :, h * 128 : h * 128 + 128]
    for i in range(16):
        for p in range(2):
            ey[2 * i + p, 0:1, :] = c1[i, p, 1, 30:31, :]
            ey[2 * i + p, 1:2, :] = c1[i, p, 0, 31:32, :]
            ey[2 * i + p, 2:3, :] = c1[i, p, 1, 31:32, :]
            ey[2 * i + p, 3:4, :] = c1[i, p, 1, 31:32, :]


def pack(cc1, r2r, r2l, ey, parts, ahead, behind, part):
    total = jnp.sum(parts[...], axis=0, keepdims=True)
    part[...] = jnp.broadcast_to(total, part.shape)
    for k in range(15):
        ahead[k] = r2l[32 * k : 32 * k + 16, :]
        behind[16 * k : 16 * k + 16, :] = r2l[32 * k + 16 : 32 * k + 32, :]
    for k in range(16):
        ahead[k + 15] = cc1[k, 0:16, :]
        behind[240 + 16 * k : 256 + 16 * k, :] = cc1[k, 16:32, :]
    for k in range(13):
        ahead[k + 31] = r2r[k, 0:16, :]
        behind[496 + 16 * k : 512 + 16 * k, :] = r2r[k, 16:32, :]
    for k in range(34):
        for h in range(2):
            to = 704 + k * 4 + 136 * h
            if k < 3:
                src = 480 + 192 * h + 64 * k
                behind[to : to + 1, :] = r2l[src + 62 : src + 63, :]
                behind[to + 1 : to + 2, :] = r2l[src + 31 : src + 32, :]
                behind[to + 2 : to + 3, :] = r2l[src + 63 : src + 64, :]
                behind[to + 3 : to + 4, :] = r2l[src + 63 : src + 64, :]
            else:
                behind[to : to + 4, :] = ey[k - 3, :, h * 128 : h * 128 + 128]


def forward_rest(
    cc1, r2r, r2l, r2u, r2d, parts, c2, c3, total, x2, z2, x3, z3, w2h, w2l, w3h, w3l
):
    depth_weights(128, w2h, w2l)
    depth_weights(64, w3h, w3l)
    total[...] = jnp.sum(parts[...], axis=0, keepdims=True)

    def near(k):
        if k < 15:
            return r2l[32 * k : 32 * k + 32, :]
        return cc1[k - 15] if k < 31 else r2r[k - 31]

    def put(lo, hi):
        def store(i, p, v):
            x2[i, p, lo:hi, :] = v

        return store

    lift_x(raw(lambda k: r2d[16 * k : 16 * k + 16, :]), put(0, 16), 22)
    lift_x(raw(near), put(16, 48), 22)
    lift_x(raw(lambda k: r2u[k]), put(48, 64), 22)

    @pl.loop(0, 20)
    def _(i):
        for p in range(2):
            x2[i, p, 64:72, :] = jnp.zeros((8, 128), F32)
            d, s = lift_y(lambda k: x2[i, p, pl.ds(k + 1, 32, stride=2), :])
            z2[i, p, 0] = d
            z2[i, p, 1] = s

    u = times(z2[...].reshape(2560, 128), w2h, w2l)
    c2[...] = u.reshape(20, 2, 2, 32, 128)

    def put3(i, p, v):
        x3[i, p, :, :] = v

    lift_x(raw(lambda k: c2[k, 1, 1]), put3, 10)
    for i in range(8):
        for p in range(2):
            d, s = lift_y(lambda k: x3[i, p, pl.ds(k, 12, stride=2), :])
            z3[i, p, 0, 0:4, :] = jnp.zeros((4, 128), F32)
            z3[i, p, 0, 4:16, :] = d
            z3[i, p, 1, 0:4, :] = jnp.zeros((4, 128), F32)
            z3[i, p, 1, 4:16, :] = s
    u = times(z3[...].reshape(512, 128), w3h, w3l)
    c3[...] = u.reshape(8, 2, 2, 16, 128)


def left_one(r2l, k):
    lo = r2l[480 + 64 * k : 544 + 64 * k, :]
    hi = r2l[672 + 64 * k : 736 + 64 * k, :]
    return jnp.concatenate([lo, hi], axis=1).reshape(2, 32, 256)


def inverse_all(
    c1, c2, c3, r2l, r2d, total, out,
    u3, y3, z3, u2, y2, z2, dd, ss, y1, z1, sent,
    w1h, w1l, w2h, w2l, w3h, w3l, *, factor
):
    depth_weights(256, w1h, w1l)
    depth_weights(128, w2h, w2l)
    depth_weights(64, w3h, w3l)
    noise = total[...] * factor
    wide = jnp.concatenate([noise, noise], axis=1)
    scale = {(0, 0): 1.0 / DD, (0, 1): 1.0, (1, 0): 1.0, (1, 1): DD}

    for i in range(8):
        for p in range(2):
            for q in range(2):
                t = noise * (scale[p, q] * DD * DD)
                c = c3[i, p, q]
                kept = shrink(c, t)
                if p and q:
                    low = lax.broadcasted_iota(jnp.int32, (16, 128), 1) < 32
                    kept = jnp.where(low, c, kept)
                u3[i, p, q] = kept
            e, o = unlift(
                u3[i, p, 0, 5:15, :],
                u3[i, p, 0, 6:16, :],
                u3[i, p, 1, 4:14, :],
                u3[i, p, 1, 5:15, :],
            )
            y3[i, p, 0:4, :] = jnp.zeros((4, 128), F32)
            y3[i, p, pl.ds(4, 10, stride=2), :] = e
            y3[i, p, pl.ds(5, 10, stride=2), :] = o

    def put3(k, v):
        z3[k * 24 : k * 24 + 24, :] = v

    unlift_x(lambda m, p: y3[m, p], put3, 8)
    rb2 = times(z3[...], w3h, w3l, True).reshape(12, 24, 128)

    for i in range(12):
        for p in range(2):
            for q in range(2):
                t = noise * (scale[p, q] * DD)
                u2[i, p, q] = shrink(c2[i + 4, p, q, 0:24, :], t)
            if p:
                u2[i, 1, 1, :, 0:64] = rb2[i][:, 0:64]
            e, o = unlift(
                u2[i, p, 0, 5:23, :],
                u2[i, p, 0, 6:24, :],
                u2[i, p, 1, 4:22, :],
                u2[i, p, 1, 5:23, :],
            )
            y2[i, p, 0:8, :] = jnp.zeros((8, 128), F32)
            y2[i, p, 40:48, :] = jnp.zeros((8, 128), F32)
            y2[i, p, pl.ds(5, 18, stride=2), :] = e
            y2[i, p, pl.ds(6, 18, stride=2), :] = o

    def put2(k, v):
        z2[k * 48 : k * 48 + 48, :] = v

    unlift_x(lambda m, p: y2[m, p], put2, 12)
    z2[...] = times(z2[...], w2h, w2l, True)

    t_d = {p: wide * scale[p, 0] for p in range(2)}
    t_s = {p: wide * scale[p, 1] for p in range(2)}

    def layer(l, p, mid_d, mid_s, cell):
        lo, hi = r2d[pl.ds(704 + l * 4, 4), :], r2d[pl.ds(840 + l * 4, 4), :]
        top = jnp.concatenate([lo, hi], axis=1)
        dd[p, 7:8, :] = shrink(top[1:2], t_d[p])
        dd[p, 8:40, :] = shrink(mid_d, t_d[p])
        ss[p, 6:7, :] = shrink(top[0:1], t_s[p])
        ss[p, 7:8, :] = shrink(top[2:3], t_s[p])
        ss[p, 8:40, :] = shrink(mid_s, t_s[p])
        if p:
            ss[p, :, 0:128] = z2[pl.ds(cell * 48, 40), :]
        e, o = unlift(
            dd[p, 7:39, :], dd[p, 8:40, :], ss[p, 6:38, :], ss[p, 7:39, :]
        )
        for h in range(2):
            y1[l, h, pl.ds(0, 32, stride=2), :] = e[:, h * 128 : h * 128 + 128]
            y1[l, h, pl.ds(1, 32, stride=2), :] = o[:, h * 128 : h * 128 + 128]

    for k in range(3):
        mid = left_one(r2l, k)
        layer(k, 1 - k % 2, mid[0], mid[1], (k - 2) // 2 + 2)

    @pl.loop(0, 15)
    def _(i):
        layer(2 * i + 3, 0, c1[i, 0, 0], c1[i, 0, 1], None)
        layer(2 * i + 4, 1, c1[i, 1, 0], c1[i, 1, 1], i + 3)

    layer(33, 0, c1[15, 0, 0], c1[15, 0, 1], None)

    @pl.loop(0, 4)
    def _(c):
        rows = pl.ds(pl.multiple_of(c * 16, 16), 16)

        for h in range(2):

            def load(m, p):
                return y1[2 * m - 1 + p, h, rows, :]

            def put(k, v):
                z1[k, rows, h * 128 : h * 128 + 128] = v

            unlift_x(load, put, 18)

    def send(g):
        rows = pl.ds(g * 8, 8)
        return pltpu.make_async_copy(z1.at[rows], out.at[rows], sent.at[g])

    @pl.loop(0, 4)
    def _(g):
        u = times(z1[pl.ds(g * 8, 8)].reshape(512, 256), w1h, w1l, True)
        z1[pl.ds(g * 8, 8)] = u.reshape(8, 64, 256)
        send(g).start()

    for g in range(4):
        send(g).wait()


def call(body, outs, scratch, args, mib, in_space=VMEM, out_space=VMEM):
    scratch = [pltpu.VMEM(s, F32) if isinstance(s, tuple) else s for s in scratch]
    return pl.pallas_call(
        body,
        out_shape=[jax.ShapeDtypeStruct(s, F32) for s in outs],
        in_specs=[in_space] * len(args),
        out_specs=[out_space] * len(outs),
        scratch_shapes=scratch,
        compiler_params=pltpu.CompilerParams(vmem_limit_bytes=mib << 20),
    )(*args)


def shared(v, axis):
    return lax.all_to_all(v, axis, 0, 0, tiled=True)


def from_ahead(v, axis):
    n = lax.axis_size(axis)
    return lax.ppermute(v, axis, [((i + 1) % n, i) for i in range(n)])


def from_behind(v, axis):
    n = lax.axis_size(axis)
    return lax.ppermute(v, axis, [(i, (i + 1) % n) for i in range(n)])


def from_corner(v):
    nx, ny = lax.axis_size("gx"), lax.axis_size("gy")
    route = [
        ((i + 1) % nx * ny + (j + 1) % ny, i * ny + j)
        for i in range(nx)
        for j in range(ny)
    ]
    return lax.ppermute(v, ("gx", "gy"), route)


def on_device(volume):
    nx, ny = lax.axis_size("gx"), lax.axis_size("gy")
    wide = [pltpu.VMEM((256, 256), BF16)] * 2
    slim = [pltpu.VMEM((128, 128), BF16)] * 2
    s, q = raw(lambda k: volume[k])(0)
    mx = jnp.stack([s, q, raw(lambda k: volume[k])(1)[1]])
    my = volume[:, 0:4]
    md = mx[:, 0:4]
    hd = from_corner(md)
    hx = from_ahead(mx, "gx")
    hy = from_ahead(my, "gy")
    (zc,) = call(depth_one, [volume.shape], wide, [volume], 8)
    c1, cc1, ahead, behind, part, ey = call(
        forward_one,
        [
            (16, 2, 2, 32, 256), (16, 32, 128), (13, 32, 128), (864, 128),
            (ny, 128), (32, 4, 256),
        ],
        [(16, 2, 2, 72, 128), (3, 64, 256), (144, 256), *wide],
        [zc, hx, hy, hd],
        16,
    )
    r2l = from_behind(behind, "gx")
    r2r = from_ahead(ahead, "gx")
    parts = shared(part, "gy")
    ahead, behind, part = call(
        pack,
        [(44, 16, 128), (976, 128), (nx, 128)],
        [],
        [cc1, r2r, r2l, ey, parts],
        4,
    )
    r2d = from_behind(behind, "gy")
    r2u = from_ahead(ahead, "gy")
    parts = shared(part, "gx")
    c2, c3, total = call(
        forward_rest,
        [(20, 2, 2, 32, 128), (8, 2, 2, 16, 128), (1, 128)],
        [(20, 2, 72, 128), (20, 2, 2, 32, 128), (8, 2, 32, 128), (8, 2, 2, 16, 128), *slim, *slim],
        [cc1, r2r, r2l, r2u, r2d, parts],
        10,
    )
    count = nx * ny * volume.size // 8
    factor = math.sqrt(math.pi / 2.0) / count * DD

    def body(*refs):
        inverse_all(*refs, factor=factor)

    (out,) = call(
        body,
        [volume.shape],
        [
            (8, 2, 2, 16, 128), (8, 2, 24, 128), (288, 128),
            (12, 2, 2, 24, 128), (12, 2, 48, 128), (960, 128),
            (2, 40, 256), (2, 40, 256), (34, 2, 64, 128), (32, 64, 256),
            pltpu.SemaphoreType.DMA((4,)), *wide, *slim, *slim,
        ],
        [c1, c2, c3, r2l, r2d, total],
        16,
        out_space=HBM,
    )
    return out


def solution(mesh):
    return jax.shard_map(
        on_device,
        mesh=mesh,
        in_specs=(P("gx", "gy", None),),
        out_specs=P("gx", "gy", None),
        check_vma=False,
    )
```

time: 91.2 us -> 54.2 us (0.59)
  the two profiles are of different devices: /device:TPU:30 before, /device:TPU:2 now
where the time goes in v1:
time: 54.2 us; the launch traced here: 53.9 us
  blocking collectives  23.8 us (44%)
  starting transfers between devices  16.3 us (30%)
  Pallas kernels  10.1 us (19%)
  local copies, waits for them, and re-layouts  2.56 us (5%)
  other arithmetic  0.97 us (2%)
    all_to_all x2, blocking collectives, shared(): return lax.all_to_all(v, axis, 0, 0, tiled=True)  23.8 us
    ppermute x4, starting transfers between devices, from_ahead(): return lax.ppermute(v, axis, [((i + 1) % n, i) for i in range(n)])  10.6 us
    pallas_call x5, Pallas kernels, call(): pl.pallas_call(body, out_shape=[jax.ShapeDtypeStruct(s, F32) for s in out...  10.1 us
    ppermute x1, starting transfers between devices, from_corner(): return lax.ppermute(v, ('gx', 'gy'), route)  5.6 us
    unnamed x2, local copies, waits for them, and re-layouts  1.59 us
  transfers between devices with their start and end apart: 7, of which 0 were waited for; matrix products, arithmetic and copies ran while one was open for 2% of the time, Pallas kernels for 3%

profile of v1, /device:TPU:2, one launch (start us, length us, event | category | flops | bytes accessed | tf_op | source)
XLA Modules:
  0.0 53.9 jit_solution(12917161231356315582)
XLA Ops:
  0.0 1.0 %multiply_subtract_fusion.1 = (f32[1,64,256]{2,1,0:T(8,128)S(1)}, f32[1,64,256]{2,1,0:T(8,128)S(1)}, f32[1,64,256]{2,1,0:T(8,128)S(1)}) fusion(f32[32,64,256]{2,1,0:T(8,128)} %vol.1), kind=kLoop, calls=%fused_computation.2 | loop fusion | flops 131072 | bytes 458752 | tf_op jit(solution)/shard_map/sub | solution.py:54
  1.0 2.3 %collective-permute-start = (f32[3,64,256]{2,1,0:T(8,128)S(1)}, f32[3,64,256]{2,1,0:T(8,128)S(1)}, u32[]{:S(2)}, u32[]{:S(2)}) collective-permute-start(f32[3,64,256]{2,1,0:T(8,128)S(1)} %pad_maximum_fusion), channel_id=1, source_target_pairs={{16,0},{32,16},{48,32},{64,48},{80,64},{96,80},{112,96},{128,112},... | collective-permute-start | bytes 589832 | tf_op jit(solution)/shard_map/ppermute | solution.py:400
  3.3 1.0 %slice.22 = f32[32,4,256]{2,1,0:T(4,128)S(1)} slice(f32[32,64,256]{2,1,0:T(8,128)} %vol.1), slice={[0:32], [0:4], [0:256]} | slice | bytes 262144 | tf_op jit(solution)/shard_map/slice | solution.py:424
  4.3 3.3 %collective-permute-start.1 = (f32[32,4,256]{2,1,0:T(4,128)S(1)}, f32[32,4,256]{2,1,0:T(4,128)S(1)}, u32[]{:S(2)}, u32[]{:S(2)}) collective-permute-start(f32[32,4,256]{2,1,0:T(4,128)S(1)} %slice.22), channel_id=1, source_target_pairs={{1,0},{2,1},{3,2},{4,3},{5,4},{6,5},{7,6},{8,7},{9,8},{10,9},{11,1... | collective-permute-start | bytes 393224 | tf_op jit(solution)/shard_map/ppermute | solution.py:400
  7.6 5.6 %collective-permute-start.2 = (f32[3,4,256]{2,1,0:T(4,128)S(1)}, f32[3,4,256]{2,1,0:T(4,128)S(1)}, u32[]{:S(2)}, u32[]{:S(2)}) collective-permute-start(f32[3,4,256]{2,1,0:T(4,128)S(1)} %slice.24), channel_id=1, source_target_pairs={{17,0},{18,1},{19,2},{20,3},{21,4},{22,5},{23,6},{24,7},{25,8},{26... | collective-permute-start | bytes 36872 | tf_op jit(solution)/shard_map/ppermute | solution.py:415
  13.2 1.6 %copy-done = f32[32,64,256]{2,1,0:T(8,128)S(1)} copy-done((f32[32,64,256]{2,1,0:T(8,128)S(1)}, f32[32,64,256]{2,1,0:T(8,128)}, u32[]{:S(2)}) %copy-start) | copy-done | bytes 2097176
  14.8 1.6 %shard_map.17.zc = f32[32,64,256]{2,1,0:T(8,128)S(1)} custom-call(f32[32,64,256]{2,1,0:T(8,128)S(1)} %copy-done), custom_call_target="tpu_custom_call" | custom-call | tf_op jit(solution)/shard_map/pallas_call | solution.py:384
  16.4 0.0 collective-permute-done.2.hd
  16.4 0.0 collective-permute-done.1.hy
  16.4 0.0 collective-permute-done.hx
  16.4 1.6 %shard_map.18 = (f32[16,2,2,32,256]{4,3,2,1,0:T(8,128)S(1)}, f32[16,32,128]{2,1,0:T(8,128)S(1)}, f32[13,32,128]{2,1,0:T(8,128)S(1)}, f32[864,128]{1,0:T(8,128)S(...) custom-call(f32[32,64,256]{2,1,0:T(8,128)S(1)} %shard_map.17.zc, f32[3,64,256]{2,1,0:T(8,128)S(1)} %collective-permute-done.hx, ...), custom_call_target="tpu_custom_call" | custom-call | tf_op jit(solution)/shard_map/pallas_call | solution.py:384
  18.1 0.1 collective-permute-start.4
  18.2 2.0 %collective-permute-start.3 = (f32[13,32,128]{2,1,0:T(8,128)S(1)}, f32[13,32,128]{2,1,0:T(8,128)S(1)}, u32[]{:S(2)}, u32[]{:S(2)}) collective-permute-start(f32[13,32,128]{2,1,0:T(8,128)S(1)} %get-tuple-element.19), channel_id=1, source_target_pairs={{16,0},{32,16},{48,32},{64,48},{80,64},{96,80},{112,96},{128,112},... | collective-permute-start | bytes 638984 | tf_op jit(solution)/shard_map/ppermute | solution.py:400
  20.2 10.7 %all_to_all.22 = f32[16,1,128]{2,1,0:T(1,128)S(1)} all-to-all(f32[16,1,128]{2,1,0:T(1,128)S(1)} %bitcast.10), channel_id=1, replica_groups=mesh['gx'=16,'gy'=16] {'gy'}, dimensions={0} | all-to-all | bytes 16384 | tf_op jit(solution)/shard_map/all_to_all | solution.py:395
  30.9 0.0 collective-permute-done.3.r2r
  30.9 0.0 collective-permute-done.4.r2l.refs_3_
  30.9 0.1 shard_map.19
  30.9 0.0 collective-permute-start.6
  31.0 2.9 %collective-permute-start.5 = (f32[44,16,128]{2,1,0:T(8,128)S(1)}, f32[44,16,128]{2,1,0:T(8,128)S(1)}, u32[]{:S(2)}, u32[]{:S(2)}) collective-permute-start(f32[44,16,128]{2,1,0:T(8,128)S(1)} %get-tuple-element.23), channel_id=1, source_target_pairs={{1,0},{2,1},{3,2},{4,3},{5,4},{6,5},{7,6},{8,7},{9,8},{10,9},{11,1... | collective-permute-start | bytes 1081352 | tf_op jit(solution)/shard_map/ppermute | solution.py:400
  33.9 13.2 %all_to_all.23 = f32[16,1,128]{2,1,0:T(1,128)S(1)} all-to-all(f32[16,1,128]{2,1,0:T(1,128)S(1)} %bitcast.11), channel_id=1, replica_groups=mesh['gx'=16,'gy'=16] {'gx'}, dimensions={0} | all-to-all | bytes 16384 | tf_op jit(solution)/shard_map/all_to_all | solution.py:395
  47.1 0.0 collective-permute-done.5.r2u
  47.1 0.0 collective-permute-done.6.r2d.refs_4_
  47.1 1.9 %shard_map.20 = (f32[20,2,2,32,128]{4,3,2,1,0:T(8,128)S(1)}, f32[8,2,2,16,128]{4,3,2,1,0:T(8,128)S(1)}, f32[1,128]{1,0:T(1,128)S(1)}) custom-call(f32[16,32,128]{2,1,0:T(8,128)S(1)} %get-tuple-element.18.cc1, f32[13,32,128]{2,1,0:T(8,128)S(1)} %collective-permute-done.3.r2r, f32[864,128]{1,0:T(8,128)S(1)} %collective-permute-done.4.r2l.refs_3_, ...), custom_call_target="tpu_custom_call" | custom-call | tf_op jit(solution)/shard_map/pallas_call | solution.py:384
  49.0 4.9 %shard_map.21 = f32[32,64,256]{2,1,0:T(8,128)} custom-call(f32[16,2,2,32,256]{4,3,2,1,0:T(8,128)S(1)} %get-tuple-element.17.refs_0_, f32[20,2,2,32,128]{4,3,2,1,0:T(8,128)S(1)} %get-tuple-element.26.refs_1_, f32[8,2,2,16,128]{4,3,2,1,0:T(8,128)S(1)} %get-tuple-element.27.refs_2_, f32[864,128]{1,0:T(8,128)S(1)} %collective-permute-done.4.r2l.refs_3_, ...), custom_call_target="tpu_custom_call" | custom-call | tf_op jit(solution)/shard_map/pallas_call | solution.py:384
  (3 shorter events, 0.0 us)
Async XLA Ops:
  1.0 15.5 %collective-permute-start = (f32[3,64,256]{2,1,0:T(8,128)S(1)}, f32[3,64,256]{2,1,0:T(8,128)S(1)}, u32[]{:S(2)}, u32[]{:S(2)}) collective-permute-start(f32[3,64,256]{2,1,0:T(8,128)S(1)} %pad_maximum_fusion), channel_id=1, source_target_pairs={{16,0},{32,16},{48,32},{64,48},{80,64},{96,80},{112,96},{128,112},... | collective-permute-start | bytes 589832 | tf_op jit(solution)/shard_map/ppermute | solution.py:400
  4.3 12.2 %collective-permute-start.1 = (f32[32,4,256]{2,1,0:T(4,128)S(1)}, f32[32,4,256]{2,1,0:T(4,128)S(1)}, u32[]{:S(2)}, u32[]{:S(2)}) collective-permute-start(f32[32,4,256]{2,1,0:T(4,128)S(1)} %slice.22), channel_id=1, source_target_pairs={{1,0},{2,1},{3,2},{4,3},{5,4},{6,5},{7,6},{8,7},{9,8},{10,9},{11,1... | collective-permute-start | bytes 393224 | tf_op jit(solution)/shard_map/ppermute | solution.py:400
  7.6 8.8 %collective-permute-start.2 = (f32[3,4,256]{2,1,0:T(4,128)S(1)}, f32[3,4,256]{2,1,0:T(4,128)S(1)}, u32[]{:S(2)}, u32[]{:S(2)}) collective-permute-start(f32[3,4,256]{2,1,0:T(4,128)S(1)} %slice.24), channel_id=1, source_target_pairs={{17,0},{18,1},{19,2},{20,3},{21,4},{22,5},{23,6},{24,7},{25,8},{26... | collective-permute-start | bytes 36872 | tf_op jit(solution)/shard_map/ppermute | solution.py:415
  13.2 1.6 %copy-start = (f32[32,64,256]{2,1,0:T(8,128)S(1)}, f32[32,64,256]{2,1,0:T(8,128)}, u32[]{:S(2)}) copy-start(f32[32,64,256]{2,1,0:T(8,128)} %vol.1) | copy-start | bytes 6291460
  18.1 12.8 %collective-permute-start.4 = (f32[864,128]{1,0:T(8,128)S(1)}, f32[864,128]{1,0:T(8,128)S(1)}, u32[]{:S(2)}, u32[]{:S(2)}) collective-permute-start(f32[864,128]{1,0:T(8,128)S(1)} %get-tuple-element.20), channel_id=1, source_target_pairs={{0,16},{16,32},{32,48},{48,64},{64,80},{80,96},{96,112},{112,128},... | collective-permute-start | bytes 1327112 | tf_op jit(solution)/shard_map/ppermute | solution.py:405
  18.2 12.7 %collective-permute-start.3 = (f32[13,32,128]{2,1,0:T(8,128)S(1)}, f32[13,32,128]{2,1,0:T(8,128)S(1)}, u32[]{:S(2)}, u32[]{:S(2)}) collective-permute-start(f32[13,32,128]{2,1,0:T(8,128)S(1)} %get-tuple-element.19), channel_id=1, source_target_pairs={{16,0},{32,16},{48,32},{64,48},{80,64},{96,80},{112,96},{128,112},... | collective-permute-start | bytes 638984 | tf_op jit(solution)/shard_map/ppermute | solution.py:400
  30.9 16.1 %collective-permute-start.6 = (f32[976,128]{1,0:T(8,128)S(1)}, f32[976,128]{1,0:T(8,128)S(1)}, u32[]{:S(2)}, u32[]{:S(2)}) collective-permute-start(f32[976,128]{1,0:T(8,128)S(1)} %get-tuple-element.24), channel_id=1, source_target_pairs={{0,1},{1,2},{2,3},{3,4},{4,5},{5,6},{6,7},{7,8},{8,9},{9,10},{10,1... | collective-permute-start | bytes 1499144 | tf_op jit(solution)/shard_map/ppermute | solution.py:405
  31.0 16.1 %collective-permute-start.5 = (f32[44,16,128]{2,1,0:T(8,128)S(1)}, f32[44,16,128]{2,1,0:T(8,128)S(1)}, u32[]{:S(2)}, u32[]{:S(2)}) collective-permute-start(f32[44,16,128]{2,1,0:T(8,128)S(1)} %get-tuple-element.23), channel_id=1, source_target_pairs={{1,0},{2,1},{3,2},{4,3},{5,4},{6,5},{7,6},{8,7},{9,8},{10,9},{11,1... | collective-permute-start | bytes 1081352 | tf_op jit(solution)/shard_map/ppermute | solution.py:400

commit v2 on v1

--- a/solution.py
+++ b/solution.py
@@ -19,32 +19,52 @@
 HBM = pl.BlockSpec(memory_space=pltpu.HBM)
 
 
-def depth_weights(n, hi_ref, lo_ref):
-    shape = hi_ref.shape
-    cell = lax.broadcasted_iota(jnp.int32, shape, 0)
-    place = lax.broadcasted_iota(jnp.int32, shape, 1)
-    at = (cell - 2 * place) & (n - 1)
+def depth_weights(n, ref, back=False):
+    size = ref.shape[0] // 3
     low = {0: 1 + FAR, 1: R3 * (1 + FAR), 2: NEAR, 3: NEAR * R3 - 1}
     high = {0: -NEAR, 1: 1 - NEAR * R3, n - 2: -FAR, n - 1: -FAR * R3}
-    w = jnp.zeros(shape, F32)
-    for k, v in low.items():
-        w = jnp.where((at == k) & (place < n // 2), K0 * v, w)
-    for k, v in high.items():
-        w = jnp.where((at == k) & (place >= n // 2), K1 * v, w)
-    if shape[0] > n:
-        w = jnp.where((cell < n) & (place < n), w, 0.0)
-    hi = w.astype(BF16)
-    hi_ref[...] = hi
-    lo_ref[...] = (w - hi.astype(F32)).astype(BF16)
-
-
-def times(x, hi_ref, lo_ref, back=False):
+    low = {k: K0 * v for k, v in low.items()}
+    high = {k: K1 * v for k, v in high.items()}
+
+    def block(shape, row, col, kinds):
+        cell = row + lax.broadcasted_iota(jnp.int32, shape, 0)
+        place = col + lax.broadcasted_iota(jnp.int32, shape, 1)
+        if back:
+            cell, place = place, cell
+        at = (cell - 2 * place) & (n - 1)
+        parts = []
+        for kind in kinds:
+            w = jnp.zeros(shape, F32)
+            for k, v in kind.items():
+                w = jnp.where(at == k, v, w)
+            parts.append(w)
+        w = parts[0]
+        if len(parts) > 1:
+            w = jnp.where(place < n // 2, w, parts[1])
+        if size > n:
+            w = jnp.where((cell < n) & (place < n), w, 0.0)
+        return w
+
+    def save(row, col, w):
+        hi = w.astype(BF16)
+        lo = (w - hi.astype(F32)).astype(BF16)
+        rows, cols = w.shape
+        for base, v in ((0, hi), (size, hi), (2 * size, lo)):
+            ref[base + row : base + row + rows, col : col + cols] = v
+
+    if n == 256:
+        for half, kind in ((0, low), (128, high)):
+            shape, at = ((128, 256), (half, 0)) if back else ((256, 128), (0, half))
+            save(*at, block(shape, *at, (kind,)))
+    else:
+        save(0, 0, block((size, size), 0, 0, (low, high)))
+
+
+def times(x, w_ref):
     hi = x.astype(BF16)
     lo = (x - hi.astype(F32)).astype(BF16)
-    w, v = hi_ref[...], lo_ref[...]
-    dims = (((1,), (1 if back else 0,)), ((), ()))
-    dot = lambda p, q: lax.dot_general(p, q, dims, preferred_element_type=F32)
-    return dot(hi, w) + (dot(lo, w) + dot(hi, v))
+    x = jnp.concatenate([hi, lo, hi], axis=1)
+    return jnp.dot(x, w_ref[...], preferred_element_type=F32)
 
 
 def raw(cell):
@@ -79,10 +99,14 @@
     return d1, s1 - d2
 
 
-def unlift(d0, d1, sm, s0):
-    first = s0 + d1
-    o = d0 + NEAR * first + FAR * (sm + d0)
+def unlift(d0, first, before):
+    o = d0 + NEAR * first + FAR * before
     return first - R3 * o, o
+
+
+def unlift_rows(d, s):
+    first = s + pltpu.roll(d, d.shape[0] - 1, 0)
+    return unlift(d, first, pltpu.roll(first, 1, 0))
 
 
 def unlift_x(load, store, pairs):
@@ -101,24 +125,24 @@
     return c - jnp.clip(c, -t, t)
 
 
-def depth_one(vol, zc, wh, wl):
-    depth_weights(256, wh, wl)
-
-    @pl.loop(0, 4)
-    def _(g):
-        u = times(vol[pl.ds(g * 8, 8)].reshape(512, 256), wh, wl)
-        zc[pl.ds(g * 8, 8)] = u.reshape(8, 64, 256)
+def depth_one(vol, zc, wf, wb):
+    depth_weights(256, wf)
+    depth_weights(256, wb, True)
+
+    for g in range(4):
+        rows = slice(g * 8, g * 8 + 8)
+        u = times(vol[rows].reshape(512, 256), wf)
+        zc[rows] = u.reshape(8, 64, 256)
 
 
 def forward_one(
-    zc, hx, hy, hd, c1, cc1, ahead, behind, part, ey, ext, hxz, hyz, wh, wl
+    zc, hx, hy, hd, wf, c1, cc1, ahead, behind, part, ey, ext, hxz, hyz
 ):
-    depth_weights(256, wh, wl)
     for k in range(35):
         hyz[4 * k : 4 * k + 4, :] = hy[k] if k < 32 else hd[k - 32]
     hyz[140:144, :] = jnp.zeros((4, 256), F32)
-    hxz[...] = times(hx[...].reshape(192, 256), wh, wl).reshape(3, 64, 256)
-    hyz[...] = times(hyz[...], wh, wl)
+    hxz[...] = times(hx[...].reshape(192, 256), wf).reshape(3, 64, 256)
+    hyz[...] = times(hyz[...], wf)
 
     def spread(cell, edge):
         inner = raw(cell)
@@ -205,10 +229,10 @@
 
 
 def forward_rest(
-    cc1, r2r, r2l, r2u, r2d, parts, c2, c3, total, x2, z2, x3, z3, w2h, w2l, w3h, w3l
+    cc1, r2r, r2l, r2u, r2d, parts, c2, s2, c3, total, x2, z2, x3, z3, w2, w3
 ):
-    depth_weights(128, w2h, w2l)
-    depth_weights(64, w3h, w3l)
+    depth_weights(128, w2)
+    depth_weights(64, w3)
     total[...] = jnp.sum(parts[...], axis=0, keepdims=True)
 
     def near(k):
@@ -226,21 +250,29 @@
     lift_x(raw(near), put(16, 48), 22)
     lift_x(raw(lambda k: r2u[k]), put(48, 64), 22)
 
-    @pl.loop(0, 20)
-    def _(i):
-        for p in range(2):
-            x2[i, p, 64:72, :] = jnp.zeros((8, 128), F32)
-            d, s = lift_y(lambda k: x2[i, p, pl.ds(k + 1, 32, stride=2), :])
-            z2[i, p, 0] = d
-            z2[i, p, 1] = s
-
-    u = times(z2[...].reshape(2560, 128), w2h, w2l)
-    c2[...] = u.reshape(20, 2, 2, 32, 128)
+    def lifted(i, p):
+        x2[i, p, 64:72, :] = jnp.zeros((8, 128), F32)
+        return lift_y(lambda k: x2[i, p, pl.ds(k + 1, 32, stride=2), :])
+
+    def inner(i):
+        dd, ds = lifted(i + 4, 0)
+        sd, ss = lifted(i + 4, 1)
+        at = pl.multiple_of(640 + i * 72, 8)
+        z2[pl.ds(at, 24), :] = dd[0:24]
+        z2[pl.ds(at + 24, 24), :] = ds[0:24]
+        z2[pl.ds(at + 48, 24), :] = sd[0:24]
+        z2[pl.ds(pl.multiple_of(128 + i * 32, 32), 32), :] = ss
+
+    pl.loop(0, 12)(inner)
+    for i in (0, 1, 2, 3, 16, 17, 18, 19):
+        z2[i * 32 : i * 32 + 32, :] = lifted(i, 1)[1]
+    s2[...] = times(z2[0:640, :], w2).reshape(20, 32, 128)
+    c2[...] = times(z2[640:1504, :], w2).reshape(12, 3, 24, 128)
 
     def put3(i, p, v):
         x3[i, p, :, :] = v
 
-    lift_x(raw(lambda k: c2[k, 1, 1]), put3, 10)
+    lift_x(raw(lambda k: s2[k]), put3, 10)
     for i in range(8):
         for p in range(2):
             d, s = lift_y(lambda k: x3[i, p, pl.ds(k, 12, stride=2), :])
@@ -248,7 +280,7 @@
             z3[i, p, 0, 4:16, :] = d
             z3[i, p, 1, 0:4, :] = jnp.zeros((4, 128), F32)
             z3[i, p, 1, 4:16, :] = s
-    u = times(z3[...].reshape(512, 128), w3h, w3l)
+    u = times(z3[...].reshape(512, 128), w3)
     c3[...] = u.reshape(8, 2, 2, 16, 128)
 
 
@@ -259,66 +291,51 @@
 
 
 def inverse_all(
-    c1, c2, c3, r2l, r2d, total, out,
-    u3, y3, z3, u2, y2, z2, dd, ss, y1, z1, sent,
-    w1h, w1l, w2h, w2l, w3h, w3l, *, factor
+    c1, c2, s2, c3, r2l, r2d, total, wb, out,
+    y3, z3, y2, z2, y1, z1, sent,
+    w2, w3, *, factor
 ):
-    depth_weights(256, w1h, w1l)
-    depth_weights(128, w2h, w2l)
-    depth_weights(64, w3h, w3l)
+    depth_weights(128, w2, True)
+    depth_weights(64, w3, True)
     noise = total[...] * factor
     wide = jnp.concatenate([noise, noise], axis=1)
     scale = {(0, 0): 1.0 / DD, (0, 1): 1.0, (1, 0): 1.0, (1, 1): DD}
 
     for i in range(8):
         for p in range(2):
-            for q in range(2):
-                t = noise * (scale[p, q] * DD * DD)
-                c = c3[i, p, q]
-                kept = shrink(c, t)
-                if p and q:
-                    low = lax.broadcasted_iota(jnp.int32, (16, 128), 1) < 32
-                    kept = jnp.where(low, c, kept)
-                u3[i, p, q] = kept
-            e, o = unlift(
-                u3[i, p, 0, 5:15, :],
-                u3[i, p, 0, 6:16, :],
-                u3[i, p, 1, 4:14, :],
-                u3[i, p, 1, 5:15, :],
+            d, s = (
+                shrink(c3[i, p, q], noise * (scale[p, q] * DD * DD)) for q in range(2)
             )
-            y3[i, p, 0:4, :] = jnp.zeros((4, 128), F32)
-            y3[i, p, pl.ds(4, 10, stride=2), :] = e
-            y3[i, p, pl.ds(5, 10, stride=2), :] = o
+            if p:
+                low = lax.broadcasted_iota(jnp.int32, (16, 128), 1) < 32
+                s = jnp.where(low, c3[i, 1, 1], s)
+            e, o = unlift_rows(d, s)
+            y3[i, p, pl.ds(2, 16, stride=2), :] = e
+            y3[i, p, pl.ds(3, 16, stride=2), :] = o
 
     def put3(k, v):
         z3[k * 24 : k * 24 + 24, :] = v
 
-    unlift_x(lambda m, p: y3[m, p], put3, 8)
-    rb2 = times(z3[...], w3h, w3l, True).reshape(12, 24, 128)
+    unlift_x(lambda m, p: y3[m, p, 8:32, :], put3, 8)
+    rb2 = times(z3[...], w3).reshape(12, 24, 128)
 
     for i in range(12):
         for p in range(2):
-            for q in range(2):
-                t = noise * (scale[p, q] * DD)
-                u2[i, p, q] = shrink(c2[i + 4, p, q, 0:24, :], t)
+            d = shrink(c2[i, 2 * p], noise * (scale[p, 0] * DD))
+            s = s2[i + 4, 0:24, :] if p else c2[i, 1]
+            s = shrink(s, noise * (scale[p, 1] * DD))
             if p:
-                u2[i, 1, 1, :, 0:64] = rb2[i][:, 0:64]
-            e, o = unlift(
-                u2[i, p, 0, 5:23, :],
-                u2[i, p, 0, 6:24, :],
-                u2[i, p, 1, 4:22, :],
-                u2[i, p, 1, 5:23, :],
-            )
-            y2[i, p, 0:8, :] = jnp.zeros((8, 128), F32)
-            y2[i, p, 40:48, :] = jnp.zeros((8, 128), F32)
-            y2[i, p, pl.ds(5, 18, stride=2), :] = e
-            y2[i, p, pl.ds(6, 18, stride=2), :] = o
+                low = lax.broadcasted_iota(jnp.int32, (24, 128), 1) < 64
+                s = jnp.where(low, rb2[i], s)
+            e, o = unlift_rows(d, s)
+            y2[i, p, pl.ds(3, 24, stride=2), :] = e
+            y2[i, p, pl.ds(4, 24, stride=2), :] = o
 
     def put2(k, v):
         z2[k * 48 : k * 48 + 48, :] = v
 
-    unlift_x(lambda m, p: y2[m, p], put2, 12)
-    z2[...] = times(z2[...], w2h, w2l, True)
+    unlift_x(lambda m, p: y2[m, p, 8:56, :], put2, 12)
+    z2[...] = times(z2[...], w2)
 
     t_d = {p: wide * scale[p, 0] for p in range(2)}
     t_s = {p: wide * scale[p, 1] for p in range(2)}
@@ -326,16 +343,22 @@
     def layer(l, p, mid_d, mid_s, cell):
         lo, hi = r2d[pl.ds(704 + l * 4, 4), :], r2d[pl.ds(840 + l * 4, 4), :]
         top = jnp.concatenate([lo, hi], axis=1)
-        dd[p, 7:8, :] = shrink(top[1:2], t_d[p])
-        dd[p, 8:40, :] = shrink(mid_d, t_d[p])
-        ss[p, 6:7, :] = shrink(top[0:1], t_s[p])
-        ss[p, 7:8, :] = shrink(top[2:3], t_s[p])
-        ss[p, 8:40, :] = shrink(mid_s, t_s[p])
+        d_top = shrink(top[1:2], t_d[p])
+        s_top = shrink(top[2:3], t_s[p])
+        s_over = shrink(top[0:1], t_s[p])
+        d, s = shrink(mid_d, t_d[p]), shrink(mid_s, t_s[p])
         if p:
-            ss[p, :, 0:128] = z2[pl.ds(cell * 48, 40), :]
-        e, o = unlift(
-            dd[p, 7:39, :], dd[p, 8:40, :], ss[p, 6:38, :], ss[p, 7:39, :]
-        )
+            rebuilt = z2[pl.ds(cell * 48, 40), :]
+            s = jnp.concatenate([rebuilt[8:40], s[:, 128:]], axis=1)
+            s_top = jnp.concatenate([rebuilt[7:8], s_top[:, 128:]], axis=1)
+            s_over = jnp.concatenate([rebuilt[6:7], s_over[:, 128:]], axis=1)
+        head = lax.broadcasted_iota(jnp.int32, (32, 256), 0) == 0
+
+        def after(row, v):
+            return jnp.where(head, row, pltpu.roll(v, 1, 0))
+
+        first = after(s_top, s) + d
+        e, o = unlift(after(d_top, d), first, after(s_over + d_top, first))
         for h in range(2):
             y1[l, h, pl.ds(0, 32, stride=2), :] = e[:, h * 128 : h * 128 + 128]
             y1[l, h, pl.ds(1, 32, stride=2), :] = o[:, h * 128 : h * 128 + 128]
@@ -366,24 +389,23 @@
             unlift_x(load, put, 18)
 
     def send(g):
-        rows = pl.ds(g * 8, 8)
+        rows = pl.ds(g * 4, 4)
         return pltpu.make_async_copy(z1.at[rows], out.at[rows], sent.at[g])
 
-    @pl.loop(0, 4)
-    def _(g):
-        u = times(z1[pl.ds(g * 8, 8)].reshape(512, 256), w1h, w1l, True)
-        z1[pl.ds(g * 8, 8)] = u.reshape(8, 64, 256)
+    for g in range(8):
+        u = times(z1[pl.ds(g * 4, 4)].reshape(256, 256), wb)
+        z1[pl.ds(g * 4, 4)] = u.reshape(4, 64, 256)
         send(g).start()
 
-    for g in range(4):
+    for g in range(8):
         send(g).wait()
 
 
-def call(body, outs, scratch, args, mib, in_space=VMEM, out_space=VMEM):
+def call(body, outs, scratch, args, mib, in_space=VMEM, out_space=VMEM, kinds=None):
     scratch = [pltpu.VMEM(s, F32) if isinstance(s, tuple) else s for s in scratch]
     return pl.pallas_call(
         body,
-        out_shape=[jax.ShapeDtypeStruct(s, F32) for s in outs],
+        out_shape=[jax.ShapeDtypeStruct(*v) for v in zip(outs, kinds or [F32] * len(outs))],
         in_specs=[in_space] * len(args),
         out_specs=[out_space] * len(outs),
         scratch_shapes=scratch,
@@ -417,43 +439,44 @@
 
 def on_device(volume):
     nx, ny = lax.axis_size("gx"), lax.axis_size("gy")
-    wide = [pltpu.VMEM((256, 256), BF16)] * 2
-    slim = [pltpu.VMEM((128, 128), BF16)] * 2
+    slim = [pltpu.VMEM((384, 128), BF16)] * 2
     s, q = raw(lambda k: volume[k])(0)
     mx = jnp.stack([s, q, raw(lambda k: volume[k])(1)[1]])
-    my = volume[:, 0:4]
     md = mx[:, 0:4]
     hd = from_corner(md)
     hx = from_ahead(mx, "gx")
-    hy = from_ahead(my, "gy")
-    (zc,) = call(depth_one, [volume.shape], wide, [volume], 8)
+    hy = from_ahead(volume[:, 0:4], "gy")
+    zc, wf, wb = call(
+        depth_one,
+        [volume.shape, (768, 256), (768, 256)],
+        [],
+        [volume],
+        8,
+        kinds=[F32, BF16, BF16],
+    )
     c1, cc1, ahead, behind, part, ey = call(
         forward_one,
         [
             (16, 2, 2, 32, 256), (16, 32, 128), (13, 32, 128), (864, 128),
             (ny, 128), (32, 4, 256),
         ],
-        [(16, 2, 2, 72, 128), (3, 64, 256), (144, 256), *wide],
-        [zc, hx, hy, hd],
+        [(16, 2, 2, 72, 128), (3, 64, 256), (144, 256)],
+        [zc, hx, hy, hd, wf],
         16,
     )
     r2l = from_behind(behind, "gx")
     r2r = from_ahead(ahead, "gx")
     parts = shared(part, "gy")
     ahead, behind, part = call(
-        pack,
-        [(44, 16, 128), (976, 128), (nx, 128)],
-        [],
-        [cc1, r2r, r2l, ey, parts],
-        4,
+        pack, [(44, 16, 128), (976, 128), (nx, 128)], [], [cc1, r2r, r2l, ey, parts], 4
     )
     r2d = from_behind(behind, "gy")
     r2u = from_ahead(ahead, "gy")
     parts = shared(part, "gx")
-    c2, c3, total = call(
+    c2, s2, c3, total = call(
         forward_rest,
-        [(20, 2, 2, 32, 128), (8, 2, 2, 16, 128), (1, 128)],
-        [(20, 2, 72, 128), (20, 2, 2, 32, 128), (8, 2, 32, 128), (8, 2, 2, 16, 128), *slim, *slim],
+        [(12, 3, 24, 128), (20, 32, 128), (8, 2, 2, 16, 128), (1, 128)],
+        [(20, 2, 72, 128), (1504, 128), (8, 2, 32, 128), (8, 2, 2, 16, 128), *slim],
         [cc1, r2r, r2l, r2u, r2d, parts],
         10,
     )
@@ -467,12 +490,11 @@
         body,
         [volume.shape],
         [
-            (8, 2, 2, 16, 128), (8, 2, 24, 128), (288, 128),
-            (12, 2, 2, 24, 128), (12, 2, 48, 128), (960, 128),
-            (2, 40, 256), (2, 40, 256), (34, 2, 64, 128), (32, 64, 256),
-            pltpu.SemaphoreType.DMA((4,)), *wide, *slim, *slim,
+            (8, 2, 40, 128), (288, 128), (12, 2, 56, 128), (960, 128),
+            (34, 2, 64, 128), (32, 64, 256),
+            pltpu.SemaphoreType.DMA((8,)), *slim,
         ],
-        [c1, c2, c3, r2l, r2d, total],
+        [c1, c2, s2, c3, r2l, r2d, total, wb],
         16,
         out_space=HBM,
     )

time: 54.2 us -> 52.2 us (0.963)
  Pallas kernels: 10.1 us -> 7.77 us
    pallas_call x5, Pallas kernels: 10.1 us -> 7.77 us  [call(): pl.pallas_call(body, out_shape=[jax.ShapeDtypeStruct(*v) for v in zip(out...]
  transfers between devices with their start and end apart: 7 -> 7, of which waited for: 0 -> 0; matrix products, arithmetic and copies ran while one was open for 2% -> 2% of each run, Pallas kernels for 3% -> 2%
where the time goes in v2:
time: 52.2 us; the launch traced here: 51.9 us
  blocking collectives  24.2 us (46%)
  starting transfers between devices  16.3 us (31%)
  Pallas kernels  7.77 us (15%)
  local copies, waits for them, and re-layouts  2.56 us (5%)
  other arithmetic  0.97 us (2%)
    all_to_all x2, blocking collectives, shared(): return lax.all_to_all(v, axis, 0, 0, tiled=True)  24.2 us
    ppermute x4, starting transfers between devices, from_ahead(): return lax.ppermute(v, axis, [((i + 1) % n, i) for i in range(n)])  10.6 us
    pallas_call x5, Pallas kernels, call(): pl.pallas_call(body, out_shape=[jax.ShapeDtypeStruct(*v) for v in zip(out...  7.77 us
    ppermute x1, starting transfers between devices, from_corner(): return lax.ppermute(v, ('gx', 'gy'), route)  5.6 us
    unnamed x2, local copies, waits for them, and re-layouts  1.59 us
  transfers between devices with their start and end apart: 7, of which 0 were waited for; matrix products, arithmetic and copies ran while one was open for 2% of the time, Pallas kernels for 2%

profile of v2, /device:TPU:2, one launch (start us, length us, event | category | flops | bytes accessed | tf_op | source)
XLA Modules:
  0.0 51.9 jit_solution(14905288692295469261)
XLA Ops:
  0.0 1.0 %multiply_subtract_fusion.1 = (f32[1,64,256]{2,1,0:T(8,128)S(1)}, f32[1,64,256]{2,1,0:T(8,128)S(1)}, f32[1,64,256]{2,1,0:T(8,128)S(1)}) fusion(f32[32,64,256]{2,1,0:T(8,128)} %vol.1), kind=kLoop, calls=%fused_computation.2 | loop fusion | flops 131072 | bytes 458752 | tf_op jit(solution)/shard_map/sub | solution.py:74
  1.0 2.3 %collective-permute-start = (f32[3,64,256]{2,1,0:T(8,128)S(1)}, f32[3,64,256]{2,1,0:T(8,128)S(1)}, u32[]{:S(2)}, u32[]{:S(2)}) collective-permute-start(f32[3,64,256]{2,1,0:T(8,128)S(1)} %pad_maximum_fusion), channel_id=1, source_target_pairs={{16,0},{32,16},{48,32},{64,48},{80,64},{96,80},{112,96},{128,112},... | collective-permute-start | bytes 589832 | tf_op jit(solution)/shard_map/ppermute | solution.py:422
  3.3 1.0 %slice.22 = f32[32,4,256]{2,1,0:T(4,128)S(1)} slice(f32[32,64,256]{2,1,0:T(8,128)} %vol.1), slice={[0:32], [0:4], [0:256]} | slice | bytes 262144 | tf_op jit(solution)/shard_map/slice | solution.py:448
  4.3 3.3 %collective-permute-start.1 = (f32[32,4,256]{2,1,0:T(4,128)S(1)}, f32[32,4,256]{2,1,0:T(4,128)S(1)}, u32[]{:S(2)}, u32[]{:S(2)}) collective-permute-start(f32[32,4,256]{2,1,0:T(4,128)S(1)} %slice.22), channel_id=1, source_target_pairs={{1,0},{2,1},{3,2},{4,3},{5,4},{6,5},{7,6},{8,7},{9,8},{10,9},{11,1... | collective-permute-start | bytes 393224 | tf_op jit(solution)/shard_map/ppermute | solution.py:422
  7.6 5.6 %collective-permute-start.2 = (f32[3,4,256]{2,1,0:T(4,128)S(1)}, f32[3,4,256]{2,1,0:T(4,128)S(1)}, u32[]{:S(2)}, u32[]{:S(2)}) collective-permute-start(f32[3,4,256]{2,1,0:T(4,128)S(1)} %slice.24), channel_id=1, source_target_pairs={{17,0},{18,1},{19,2},{20,3},{21,4},{22,5},{23,6},{24,7},{25,8},{26... | collective-permute-start | bytes 36872 | tf_op jit(solution)/shard_map/ppermute | solution.py:437
  13.2 1.6 %copy-done = f32[32,64,256]{2,1,0:T(8,128)S(1)} copy-done((f32[32,64,256]{2,1,0:T(8,128)S(1)}, f32[32,64,256]{2,1,0:T(8,128)}, u32[]{:S(2)}) %copy-start) | copy-done | bytes 2097176
  14.8 1.2 %shard_map.17 = (f32[32,64,256]{2,1,0:T(8,128)S(1)}, bf16[768,256]{1,0:T(8,128)(2,1)S(1)}, bf16[768,256]{1,0:T(8,128)(2,1)S(1)}) custom-call(f32[32,64,256]{2,1,0:T(8,128)S(1)} %copy-done), custom_call_target="tpu_custom_call" | custom-call | tf_op jit(solution)/shard_map/pallas_call | solution.py:406
  16.0 0.0 collective-permute-done.2.hd
  16.0 0.0 collective-permute-done.1.hy
  16.0 0.0 collective-permute-done.hx
  16.0 1.5 %shard_map.18 = (f32[16,2,2,32,256]{4,3,2,1,0:T(8,128)S(1)}, f32[16,32,128]{2,1,0:T(8,128)S(1)}, f32[13,32,128]{2,1,0:T(8,128)S(1)}, f32[864,128]{1,0:T(8,128)S(...) custom-call(f32[32,64,256]{2,1,0:T(8,128)S(1)} %get-tuple-element.21.zc, ...), custom_call_target="tpu_custom_call" | custom-call | tf_op jit(solution)/shard_map/pallas_call | solution.py:406
  17.6 0.1 collective-permute-start.4
  17.7 2.0 %collective-permute-start.3 = (f32[13,32,128]{2,1,0:T(8,128)S(1)}, f32[13,32,128]{2,1,0:T(8,128)S(1)}, u32[]{:S(2)}, u32[]{:S(2)}) collective-permute-start(f32[13,32,128]{2,1,0:T(8,128)S(1)} %get-tuple-element.25), channel_id=1, source_target_pairs={{16,0},{32,16},{48,32},{64,48},{80,64},{96,80},{112,96},{128,112},... | collective-permute-start | bytes 638984 | tf_op jit(solution)/shard_map/ppermute | solution.py:422
  19.7 10.7 %all_to_all.22 = f32[16,1,128]{2,1,0:T(1,128)S(1)} all-to-all(f32[16,1,128]{2,1,0:T(1,128)S(1)} %bitcast.10), channel_id=1, replica_groups=mesh['gx'=16,'gy'=16] {'gy'}, dimensions={0} | all-to-all | bytes 16384 | tf_op jit(solution)/shard_map/all_to_all | solution.py:417
  30.4 0.0 collective-permute-done.3.r2r
  30.4 0.0 collective-permute-done.4.r2l.refs_4_
  30.4 0.1 shard_map.19
  30.5 0.0 collective-permute-start.6
  30.5 2.9 %collective-permute-start.5 = (f32[44,16,128]{2,1,0:T(8,128)S(1)}, f32[44,16,128]{2,1,0:T(8,128)S(1)}, u32[]{:S(2)}, u32[]{:S(2)}) collective-permute-start(f32[44,16,128]{2,1,0:T(8,128)S(1)} %get-tuple-element.29), channel_id=1, source_target_pairs={{1,0},{2,1},{3,2},{4,3},{5,4},{6,5},{7,6},{8,7},{9,8},{10,9},{11,1... | collective-permute-start | bytes 1081352 | tf_op jit(solution)/shard_map/ppermute | solution.py:422
  33.4 13.6 %all_to_all.23 = f32[16,1,128]{2,1,0:T(1,128)S(1)} all-to-all(f32[16,1,128]{2,1,0:T(1,128)S(1)} %bitcast.11), channel_id=1, replica_groups=mesh['gx'=16,'gy'=16] {'gx'}, dimensions={0} | all-to-all | bytes 16384 | tf_op jit(solution)/shard_map/all_to_all | solution.py:417
  47.0 0.0 collective-permute-done.5.r2u
  47.0 0.0 collective-permute-done.6.r2d.refs_5_
  47.0 1.1 %shard_map.20 = (f32[12,3,24,128]{3,2,1,0:T(8,128)S(1)}, f32[20,32,128]{2,1,0:T(8,128)S(1)}, f32[8,2,2,16,128]{4,3,2,1,0:T(8,128)S(1)}, f32[1,128]{1,0:T(1,128)S(1)}) custom-call(f32[16,32,128]{2,1,0:T(8,128)S(1)} %get-tuple-element.24.cc1, f32[13,32,128]{2,1,0:T(8,128)S(1)} %collective-permute-done.3.r2r, ...), custom_call_target="tpu_custom_call" | custom-call | tf_op jit(solution)/shard_map/pallas_call | solution.py:406
  48.1 3.8 %shard_map.21 = f32[32,64,256]{2,1,0:T(8,128)} custom-call(f32[16,2,2,32,256]{4,3,2,1,0:T(8,128)S(1)} %get-tuple-element.23.refs_0_, f32[12,3,24,128]{3,2,1,0:T(8,128)S(1)} %get-tuple-element.32.refs_1_, f32[20,32,128]{2,1,0:T(8,128)S(1)} %get-tuple-element.33.refs_2_, f32[8,2,2,16,128]{4,3,2,1,0:T(8,128)S(1)} %get-tuple-element.34.refs_3_, ...), custom_call_target="tpu_custom_call" | custom-call | tf_op jit(solution)/shard_map/pallas_call | solution.py:406
  (3 shorter events, 0.0 us)
Async XLA Ops:
  1.0 15.1 %collective-permute-start = (f32[3,64,256]{2,1,0:T(8,128)S(1)}, f32[3,64,256]{2,1,0:T(8,128)S(1)}, u32[]{:S(2)}, u32[]{:S(2)}) collective-permute-start(f32[3,64,256]{2,1,0:T(8,128)S(1)} %pad_maximum_fusion), channel_id=1, source_target_pairs={{16,0},{32,16},{48,32},{64,48},{80,64},{96,80},{112,96},{128,112},... | collective-permute-start | bytes 589832 | tf_op jit(solution)/shard_map/ppermute | solution.py:422
  4.3 11.8 %collective-permute-start.1 = (f32[32,4,256]{2,1,0:T(4,128)S(1)}, f32[32,4,256]{2,1,0:T(4,128)S(1)}, u32[]{:S(2)}, u32[]{:S(2)}) collective-permute-start(f32[32,4,256]{2,1,0:T(4,128)S(1)} %slice.22), channel_id=1, source_target_pairs={{1,0},{2,1},{3,2},{4,3},{5,4},{6,5},{7,6},{8,7},{9,8},{10,9},{11,1... | collective-permute-start | bytes 393224 | tf_op jit(solution)/shard_map/ppermute | solution.py:422
  7.6 8.4 %collective-permute-start.2 = (f32[3,4,256]{2,1,0:T(4,128)S(1)}, f32[3,4,256]{2,1,0:T(4,128)S(1)}, u32[]{:S(2)}, u32[]{:S(2)}) collective-permute-start(f32[3,4,256]{2,1,0:T(4,128)S(1)} %slice.24), channel_id=1, source_target_pairs={{17,0},{18,1},{19,2},{20,3},{21,4},{22,5},{23,6},{24,7},{25,8},{26... | collective-permute-start | bytes 36872 | tf_op jit(solution)/shard_map/ppermute | solution.py:437
  13.2 1.6 %copy-start = (f32[32,64,256]{2,1,0:T(8,128)S(1)}, f32[32,64,256]{2,1,0:T(8,128)}, u32[]{:S(2)}) copy-start(f32[32,64,256]{2,1,0:T(8,128)} %vol.1) | copy-start | bytes 6291460
  17.6 12.8 %collective-permute-start.4 = (f32[864,128]{1,0:T(8,128)S(1)}, f32[864,128]{1,0:T(8,128)S(1)}, u32[]{:S(2)}, u32[]{:S(2)}) collective-permute-start(f32[864,128]{1,0:T(8,128)S(1)} %get-tuple-element.26), channel_id=1, source_target_pairs={{0,16},{16,32},{32,48},{48,64},{64,80},{80,96},{96,112},{112,128},... | collective-permute-start | bytes 1327112 | tf_op jit(solution)/shard_map/ppermute | solution.py:427
  17.7 12.7 %collective-permute-start.3 = (f32[13,32,128]{2,1,0:T(8,128)S(1)}, f32[13,32,128]{2,1,0:T(8,128)S(1)}, u32[]{:S(2)}, u32[]{:S(2)}) collective-permute-start(f32[13,32,128]{2,1,0:T(8,128)S(1)} %get-tuple-element.25), channel_id=1, source_target_pairs={{16,0},{32,16},{48,32},{64,48},{80,64},{96,80},{112,96},{128,112},... | collective-permute-start | bytes 638984 | tf_op jit(solution)/shard_map/ppermute | solution.py:422
  30.5 16.5 %collective-permute-start.6 = (f32[976,128]{1,0:T(8,128)S(1)}, f32[976,128]{1,0:T(8,128)S(1)}, u32[]{:S(2)}, u32[]{:S(2)}) collective-permute-start(f32[976,128]{1,0:T(8,128)S(1)} %get-tuple-element.30), channel_id=1, source_target_pairs={{0,1},{1,2},{2,3},{3,4},{4,5},{5,6},{6,7},{7,8},{8,9},{9,10},{10,1... | collective-permute-start | bytes 1499144 | tf_op jit(solution)/shard_map/ppermute | solution.py:427
  30.5 16.5 %collective-permute-start.5 = (f32[44,16,128]{2,1,0:T(8,128)S(1)}, f32[44,16,128]{2,1,0:T(8,128)S(1)}, u32[]{:S(2)}, u32[]{:S(2)}) collective-permute-start(f32[44,16,128]{2,1,0:T(8,128)S(1)} %get-tuple-element.29), channel_id=1, source_target_pairs={{1,0},{2,1},{3,2},{4,3},{5,4},{6,5},{7,6},{8,7},{9,8},{10,9},{11,1... | collective-permute-start | bytes 1081352 | tf_op jit(solution)/shard_map/ppermute | solution.py:422

commit v3 on v2

--- a/solution.py
+++ b/solution.py
@@ -15,6 +15,13 @@
 DD = K1 * K1
 F32 = jnp.float32
 BF16 = jnp.bfloat16
+BLOCKS = [
+    (k, q, h)
+    for k in range(3)
+    for q in range(2)
+    for h in range(2)
+    if k == 1 or q == 0 or h == 1
+]
 VMEM = pl.BlockSpec(memory_space=pltpu.VMEM)
 HBM = pl.BlockSpec(memory_space=pltpu.HBM)
 
@@ -188,13 +195,14 @@
 
     acc = lax.fori_loop(0, 16, pair, jnp.zeros((32, 128), F32))
     part[...] = jnp.full(part.shape, jnp.sum(acc), F32)
-    ahead[...] = cc1[0:13]
-    behind[0:480, :] = cc1[1:16].reshape(480, 128)
-    for k, (i, p) in enumerate(((14, 1), (15, 0), (15, 1))):
-        for q in range(2):
-            for h in range(2):
-                at = 480 + 192 * h + 64 * k + 32 * q
-                behind[at : at + 32, :] = c1[i, p, q, :, h * 128 : h * 128 + 128]
+    ahead[0:11] = cc1[0:11]
+    ahead[11] = raw(lambda k: cc1[11 + k])(0)[1]
+    behind[0:32, :] = raw(lambda k: cc1[1 + k])(0)[0]
+    behind[32:448, :] = cc1[3:16].reshape(416, 128)
+    for n, (k, q, h) in enumerate(BLOCKS):
+        i, p = ((14, 1), (15, 0), (15, 1))[k]
+        at = 448 + 32 * n
+        behind[at : at + 32, :] = c1[i, p, q, :, h * 128 : h * 128 + 128]
     for i in range(16):
         for p in range(2):
             ey[2 * i + p, 0:1, :] = c1[i, p, 1, 30:31, :]
@@ -206,24 +214,25 @@
 def pack(cc1, r2r, r2l, ey, parts, ahead, behind, part):
     total = jnp.sum(parts[...], axis=0, keepdims=True)
     part[...] = jnp.broadcast_to(total, part.shape)
-    for k in range(15):
+    for k in range(14):
         ahead[k] = r2l[32 * k : 32 * k + 16, :]
         behind[16 * k : 16 * k + 16, :] = r2l[32 * k + 16 : 32 * k + 32, :]
     for k in range(16):
-        ahead[k + 15] = cc1[k, 0:16, :]
-        behind[240 + 16 * k : 256 + 16 * k, :] = cc1[k, 16:32, :]
-    for k in range(13):
-        ahead[k + 31] = r2r[k, 0:16, :]
-        behind[496 + 16 * k : 512 + 16 * k, :] = r2r[k, 16:32, :]
+        ahead[k + 14] = cc1[k, 0:16, :]
+        behind[224 + 16 * k : 240 + 16 * k, :] = cc1[k, 16:32, :]
+    for k in range(12):
+        ahead[k + 30] = r2r[k, 0:16, :]
+        behind[480 + 16 * k : 496 + 16 * k, :] = r2r[k, 16:32, :]
     for k in range(34):
         for h in range(2):
-            to = 704 + k * 4 + 136 * h
+            to = 672 + k * 4 + 136 * h
             if k < 3:
-                src = 480 + 192 * h + 64 * k
-                behind[to : to + 1, :] = r2l[src + 62 : src + 63, :]
-                behind[to + 1 : to + 2, :] = r2l[src + 31 : src + 32, :]
-                behind[to + 2 : to + 3, :] = r2l[src + 63 : src + 64, :]
-                behind[to + 3 : to + 4, :] = r2l[src + 63 : src + 64, :]
+                s_at = 448 + 32 * BLOCKS.index((k, 1, h if k == 1 else 1))
+                d_at = 448 + 32 * BLOCKS.index((k, 0, h))
+                behind[to : to + 1, :] = r2l[s_at + 30 : s_at + 31, :]
+                behind[to + 1 : to + 2, :] = r2l[d_at + 31 : d_at + 32, :]
+                behind[to + 2 : to + 3, :] = r2l[s_at + 31 : s_at + 32, :]
+                behind[to + 3 : to + 4, :] = r2l[s_at + 31 : s_at + 32, :]
             else:
                 behind[to : to + 4, :] = ey[k - 3, :, h * 128 : h * 128 + 128]
 
@@ -236,9 +245,19 @@
     total[...] = jnp.sum(parts[...], axis=0, keepdims=True)
 
     def near(k):
-        if k < 15:
+        if k < 14:
             return r2l[32 * k : 32 * k + 32, :]
-        return cc1[k - 15] if k < 31 else r2r[k - 31]
+        return cc1[k - 14] if k < 30 else r2r[k - 30]
+
+    def edged(layer):
+        inside = raw(lambda k: layer(k - 1))
+
+        def pair(m):
+            if m == 0:
+                return layer(0), None
+            return inside(m) if m < 21 else (None, layer(41))
+
+        return pair
 
     def put(lo, hi):
         def store(i, p, v):
@@ -246,9 +265,9 @@
 
         return store
 
-    lift_x(raw(lambda k: r2d[16 * k : 16 * k + 16, :]), put(0, 16), 22)
-    lift_x(raw(near), put(16, 48), 22)
-    lift_x(raw(lambda k: r2u[k]), put(48, 64), 22)
+    lift_x(edged(lambda k: r2d[16 * k : 16 * k + 16, :]), put(0, 16), 22)
+    lift_x(edged(near), put(16, 48), 22)
+    lift_x(edged(lambda k: r2u[k]), put(48, 64), 22)
 
     def lifted(i, p):
         x2[i, p, 64:72, :] = jnp.zeros((8, 128), F32)
@@ -285,9 +304,11 @@
 
 
 def left_one(r2l, k):
-    lo = r2l[480 + 64 * k : 544 + 64 * k, :]
-    hi = r2l[672 + 64 * k : 736 + 64 * k, :]
-    return jnp.concatenate([lo, hi], axis=1).reshape(2, 32, 256)
+    def half(q, h):
+        at = 448 + 32 * BLOCKS.index((k, q, h if (k, q, h) in BLOCKS else 1))
+        return r2l[at : at + 32, :]
+
+    return [jnp.concatenate([half(q, 0), half(q, 1)], axis=1) for q in range(2)]
 
 
 def inverse_all(
@@ -341,7 +362,7 @@
     t_s = {p: wide * scale[p, 1] for p in range(2)}
 
     def layer(l, p, mid_d, mid_s, cell):
-        lo, hi = r2d[pl.ds(704 + l * 4, 4), :], r2d[pl.ds(840 + l * 4, 4), :]
+        lo, hi = r2d[pl.ds(672 + l * 4, 4), :], r2d[pl.ds(808 + l * 4, 4), :]
         top = jnp.concatenate([lo, hi], axis=1)
         d_top = shrink(top[1:2], t_d[p])
         s_top = shrink(top[2:3], t_s[p])
@@ -374,25 +395,24 @@
 
     layer(33, 0, c1[15, 0, 0], c1[15, 0, 1], None)
 
-    @pl.loop(0, 4)
-    def _(c):
-        rows = pl.ds(pl.multiple_of(c * 16, 16), 16)
-
-        for h in range(2):
-
-            def load(m, p):
-                return y1[2 * m - 1 + p, h, rows, :]
-
-            def put(k, v):
-                z1[k, rows, h * 128 : h * 128 + 128] = v
-
-            unlift_x(load, put, 18)
-
     def send(g):
         rows = pl.ds(g * 4, 4)
         return pltpu.make_async_copy(z1.at[rows], out.at[rows], sent.at[g])
 
+    def ready(g):
+        for c in range(2):
+            for h in range(2):
+
+                def load(m, p):
+                    return y1[2 * (m + 2 * g) - 1 + p, h, c * 32 : c * 32 + 32, :]
+
+                def put(k, v):
+                    z1[4 * g + k, c * 32 : c * 32 + 32, h * 128 : h * 128 + 128] = v
+
+                unlift_x(load, put, 4)
+
     for g in range(8):
+        ready(g)
         u = times(z1[pl.ds(g * 4, 4)].reshape(256, 256), wb)
         z1[pl.ds(g * 4, 4)] = u.reshape(4, 64, 256)
         send(g).start()
@@ -457,7 +477,7 @@
     c1, cc1, ahead, behind, part, ey = call(
         forward_one,
         [
-            (16, 2, 2, 32, 256), (16, 32, 128), (13, 32, 128), (864, 128),
+            (16, 2, 2, 32, 256), (16, 32, 128), (12, 32, 128), (768, 128),
             (ny, 128), (32, 4, 256),
         ],
         [(16, 2, 2, 72, 128), (3, 64, 256), (144, 256)],
@@ -468,7 +488,7 @@
     r2r = from_ahead(ahead, "gx")
     parts = shared(part, "gy")
     ahead, behind, part = call(
-        pack, [(44, 16, 128), (976, 128), (nx, 128)], [], [cc1, r2r, r2l, ey, parts], 4
+        pack, [(42, 16, 128), (944, 128), (nx, 128)], [], [cc1, r2r, r2l, ey, parts], 4
     )
     r2d = from_behind(behind, "gy")
     r2u = from_ahead(ahead, "gy")

time: 52.2 us -> 51.8 us (level)
  no operation moved by 1% of the time
where the time goes in v3:
time: 51.8 us; the launch traced here: 51.6 us
  blocking collectives  24.2 us (47%)
  starting transfers between devices  16.3 us (31%)
  Pallas kernels  7.41 us (14%)
  local copies, waits for them, and re-layouts  2.56 us (5%)
  other arithmetic  0.97 us (2%)
    all_to_all x2, blocking collectives, shared(): return lax.all_to_all(v, axis, 0, 0, tiled=True)  24.2 us
    ppermute x4, starting transfers between devices, from_ahead(): return lax.ppermute(v, axis, [((i + 1) % n, i) for i in range(n)])  10.6 us
    pallas_call x5, Pallas kernels, call(): pl.pallas_call(body, out_shape=[jax.ShapeDtypeStruct(*v) for v in zip(out...  7.41 us
    ppermute x1, starting transfers between devices, from_corner(): return lax.ppermute(v, ('gx', 'gy'), route)  5.6 us
    unnamed x2, local copies, waits for them, and re-layouts  1.59 us
  transfers between devices with their start and end apart: 7, of which 0 were waited for; matrix products, arithmetic and copies ran while one was open for 2% of the time, Pallas kernels for 2%

profile of v3, /device:TPU:2, one launch (start us, length us, event | category | flops | bytes accessed | tf_op | source)
XLA Modules:
  0.0 51.6 jit_solution(9731077346319937953)
XLA Ops:
  0.0 1.0 %multiply_subtract_fusion.1 = (f32[1,64,256]{2,1,0:T(8,128)S(1)}, f32[1,64,256]{2,1,0:T(8,128)S(1)}, f32[1,64,256]{2,1,0:T(8,128)S(1)}) fusion(f32[32,64,256]{2,1,0:T(8,128)} %vol.1), kind=kLoop, calls=%fused_computation.2 | loop fusion | flops 131072 | bytes 458752 | tf_op jit(solution)/shard_map/sub | solution.py:81
  1.0 2.3 %collective-permute-start = (f32[3,64,256]{2,1,0:T(8,128)S(1)}, f32[3,64,256]{2,1,0:T(8,128)S(1)}, u32[]{:S(2)}, u32[]{:S(2)}) collective-permute-start(f32[3,64,256]{2,1,0:T(8,128)S(1)} %pad_maximum_fusion), channel_id=1, source_target_pairs={{16,0},{32,16},{48,32},{64,48},{80,64},{96,80},{112,96},{128,112},... | collective-permute-start | bytes 589832 | tf_op jit(solution)/shard_map/ppermute | solution.py:442
  3.3 1.0 %slice.22 = f32[32,4,256]{2,1,0:T(4,128)S(1)} slice(f32[32,64,256]{2,1,0:T(8,128)} %vol.1), slice={[0:32], [0:4], [0:256]} | slice | bytes 262144 | tf_op jit(solution)/shard_map/slice | solution.py:468
  4.3 3.3 %collective-permute-start.1 = (f32[32,4,256]{2,1,0:T(4,128)S(1)}, f32[32,4,256]{2,1,0:T(4,128)S(1)}, u32[]{:S(2)}, u32[]{:S(2)}) collective-permute-start(f32[32,4,256]{2,1,0:T(4,128)S(1)} %slice.22), channel_id=1, source_target_pairs={{1,0},{2,1},{3,2},{4,3},{5,4},{6,5},{7,6},{8,7},{9,8},{10,9},{11,1... | collective-permute-start | bytes 393224 | tf_op jit(solution)/shard_map/ppermute | solution.py:442
  7.6 5.6 %collective-permute-start.2 = (f32[3,4,256]{2,1,0:T(4,128)S(1)}, f32[3,4,256]{2,1,0:T(4,128)S(1)}, u32[]{:S(2)}, u32[]{:S(2)}) collective-permute-start(f32[3,4,256]{2,1,0:T(4,128)S(1)} %slice.24), channel_id=1, source_target_pairs={{17,0},{18,1},{19,2},{20,3},{21,4},{22,5},{23,6},{24,7},{25,8},{26... | collective-permute-start | bytes 36872 | tf_op jit(solution)/shard_map/ppermute | solution.py:457
  13.2 1.6 %copy-done = f32[32,64,256]{2,1,0:T(8,128)S(1)} copy-done((f32[32,64,256]{2,1,0:T(8,128)S(1)}, f32[32,64,256]{2,1,0:T(8,128)}, u32[]{:S(2)}) %copy-start) | copy-done | bytes 2097176
  14.8 1.2 %shard_map.17 = (f32[32,64,256]{2,1,0:T(8,128)S(1)}, bf16[768,256]{1,0:T(8,128)(2,1)S(1)}, bf16[768,256]{1,0:T(8,128)(2,1)S(1)}) custom-call(f32[32,64,256]{2,1,0:T(8,128)S(1)} %copy-done), custom_call_target="tpu_custom_call" | custom-call | tf_op jit(solution)/shard_map/pallas_call | solution.py:426
  16.0 0.0 collective-permute-done.2.hd
  16.0 0.0 collective-permute-done.1.hy
  16.0 0.0 collective-permute-done.hx
  16.0 1.5 %shard_map.18 = (f32[16,2,2,32,256]{4,3,2,1,0:T(8,128)S(1)}, f32[16,32,128]{2,1,0:T(8,128)S(1)}, f32[12,32,128]{2,1,0:T(8,128)S(1)}, f32[768,128]{1,0:T(8,128)S(...) custom-call(f32[32,64,256]{2,1,0:T(8,128)S(1)} %get-tuple-element.21.zc, ...), custom_call_target="tpu_custom_call" | custom-call | tf_op jit(solution)/shard_map/pallas_call | solution.py:426
  17.6 0.1 collective-permute-start.4
  17.7 2.0 %collective-permute-start.3 = (f32[12,32,128]{2,1,0:T(8,128)S(1)}, f32[12,32,128]{2,1,0:T(8,128)S(1)}, u32[]{:S(2)}, u32[]{:S(2)}) collective-permute-start(f32[12,32,128]{2,1,0:T(8,128)S(1)} %get-tuple-element.25), channel_id=1, source_target_pairs={{16,0},{32,16},{48,32},{64,48},{80,64},{96,80},{112,96},{128,112},... | collective-permute-start | bytes 589832 | tf_op jit(solution)/shard_map/ppermute | solution.py:442
  19.7 10.7 %all_to_all.22 = f32[16,1,128]{2,1,0:T(1,128)S(1)} all-to-all(f32[16,1,128]{2,1,0:T(1,128)S(1)} %bitcast.10), channel_id=1, replica_groups=mesh['gx'=16,'gy'=16] {'gy'}, dimensions={0} | all-to-all | bytes 16384 | tf_op jit(solution)/shard_map/all_to_all | solution.py:437
  30.4 0.0 collective-permute-done.3.r2r
  30.4 0.0 collective-permute-done.4.r2l.refs_4_
  30.4 0.1 shard_map.19
  30.5 0.0 collective-permute-start.6
  30.5 2.9 %collective-permute-start.5 = (f32[42,16,128]{2,1,0:T(8,128)S(1)}, f32[42,16,128]{2,1,0:T(8,128)S(1)}, u32[]{:S(2)}, u32[]{:S(2)}) collective-permute-start(f32[42,16,128]{2,1,0:T(8,128)S(1)} %get-tuple-element.29), channel_id=1, source_target_pairs={{1,0},{2,1},{3,2},{4,3},{5,4},{6,5},{7,6},{8,7},{9,8},{10,9},{11,1... | collective-permute-start | bytes 1032200 | tf_op jit(solution)/shard_map/ppermute | solution.py:442
  33.4 13.6 %all_to_all.23 = f32[16,1,128]{2,1,0:T(1,128)S(1)} all-to-all(f32[16,1,128]{2,1,0:T(1,128)S(1)} %bitcast.11), channel_id=1, replica_groups=mesh['gx'=16,'gy'=16] {'gx'}, dimensions={0} | all-to-all | bytes 16384 | tf_op jit(solution)/shard_map/all_to_all | solution.py:437
  47.0 0.0 collective-permute-done.5.r2u
  47.0 0.0 collective-permute-done.6.r2d.refs_5_
  47.0 1.1 %shard_map.20 = (f32[12,3,24,128]{3,2,1,0:T(8,128)S(1)}, f32[20,32,128]{2,1,0:T(8,128)S(1)}, f32[8,2,2,16,128]{4,3,2,1,0:T(8,128)S(1)}, f32[1,128]{1,0:T(1,128)S(1)}) custom-call(f32[16,32,128]{2,1,0:T(8,128)S(1)} %get-tuple-element.24.cc1, f32[12,32,128]{2,1,0:T(8,128)S(1)} %collective-permute-done.3.r2r, ...), custom_call_target="tpu_custom_call" | custom-call | tf_op jit(solution)/shard_map/pallas_call | solution.py:426
  48.1 3.5 %shard_map.21 = f32[32,64,256]{2,1,0:T(8,128)} custom-call(f32[16,2,2,32,256]{4,3,2,1,0:T(8,128)S(1)} %get-tuple-element.23.refs_0_, f32[12,3,24,128]{3,2,1,0:T(8,128)S(1)} %get-tuple-element.32.refs_1_, f32[20,32,128]{2,1,0:T(8,128)S(1)} %get-tuple-element.33.refs_2_, f32[8,2,2,16,128]{4,3,2,1,0:T(8,128)S(1)} %get-tuple-element.34.refs_3_, ...), custom_call_target="tpu_custom_call" | custom-call | tf_op jit(solution)/shard_map/pallas_call | solution.py:426
  (3 shorter events, 0.0 us)
Async XLA Ops:
  1.0 15.1 %collective-permute-start = (f32[3,64,256]{2,1,0:T(8,128)S(1)}, f32[3,64,256]{2,1,0:T(8,128)S(1)}, u32[]{:S(2)}, u32[]{:S(2)}) collective-permute-start(f32[3,64,256]{2,1,0:T(8,128)S(1)} %pad_maximum_fusion), channel_id=1, source_target_pairs={{16,0},{32,16},{48,32},{64,48},{80,64},{96,80},{112,96},{128,112},... | collective-permute-start | bytes 589832 | tf_op jit(solution)/shard_map/ppermute | solution.py:442
  4.3 11.8 %collective-permute-start.1 = (f32[32,4,256]{2,1,0:T(4,128)S(1)}, f32[32,4,256]{2,1,0:T(4,128)S(1)}, u32[]{:S(2)}, u32[]{:S(2)}) collective-permute-start(f32[32,4,256]{2,1,0:T(4,128)S(1)} %slice.22), channel_id=1, source_target_pairs={{1,0},{2,1},{3,2},{4,3},{5,4},{6,5},{7,6},{8,7},{9,8},{10,9},{11,1... | collective-permute-start | bytes 393224 | tf_op jit(solution)/shard_map/ppermute | solution.py:442
  7.6 8.4 %collective-permute-start.2 = (f32[3,4,256]{2,1,0:T(4,128)S(1)}, f32[3,4,256]{2,1,0:T(4,128)S(1)}, u32[]{:S(2)}, u32[]{:S(2)}) collective-permute-start(f32[3,4,256]{2,1,0:T(4,128)S(1)} %slice.24), channel_id=1, source_target_pairs={{17,0},{18,1},{19,2},{20,3},{21,4},{22,5},{23,6},{24,7},{25,8},{26... | collective-permute-start | bytes 36872 | tf_op jit(solution)/shard_map/ppermute | solution.py:457
  13.2 1.6 %copy-start = (f32[32,64,256]{2,1,0:T(8,128)S(1)}, f32[32,64,256]{2,1,0:T(8,128)}, u32[]{:S(2)}) copy-start(f32[32,64,256]{2,1,0:T(8,128)} %vol.1) | copy-start | bytes 6291460
  17.6 12.8 %collective-permute-start.4 = (f32[768,128]{1,0:T(8,128)S(1)}, f32[768,128]{1,0:T(8,128)S(1)}, u32[]{:S(2)}, u32[]{:S(2)}) collective-permute-start(f32[768,128]{1,0:T(8,128)S(1)} %get-tuple-element.26), channel_id=1, source_target_pairs={{0,16},{16,32},{32,48},{48,64},{64,80},{80,96},{96,112},{112,128},... | collective-permute-start | bytes 1179656 | tf_op jit(solution)/shard_map/ppermute | solution.py:447
  17.7 12.7 %collective-permute-start.3 = (f32[12,32,128]{2,1,0:T(8,128)S(1)}, f32[12,32,128]{2,1,0:T(8,128)S(1)}, u32[]{:S(2)}, u32[]{:S(2)}) collective-permute-start(f32[12,32,128]{2,1,0:T(8,128)S(1)} %get-tuple-element.25), channel_id=1, source_target_pairs={{16,0},{32,16},{48,32},{64,48},{80,64},{96,80},{112,96},{128,112},... | collective-permute-start | bytes 589832 | tf_op jit(solution)/shard_map/ppermute | solution.py:442
  30.5 16.5 %collective-permute-start.6 = (f32[944,128]{1,0:T(8,128)S(1)}, f32[944,128]{1,0:T(8,128)S(1)}, u32[]{:S(2)}, u32[]{:S(2)}) collective-permute-start(f32[944,128]{1,0:T(8,128)S(1)} %get-tuple-element.30), channel_id=1, source_target_pairs={{0,1},{1,2},{2,3},{3,4},{4,5},{5,6},{6,7},{7,8},{8,9},{9,10},{10,1... | collective-permute-start | bytes 1449992 | tf_op jit(solution)/shard_map/ppermute | solution.py:447
  30.5 16.5 %collective-permute-start.5 = (f32[42,16,128]{2,1,0:T(8,128)S(1)}, f32[42,16,128]{2,1,0:T(8,128)S(1)}, u32[]{:S(2)}, u32[]{:S(2)}) collective-permute-start(f32[42,16,128]{2,1,0:T(8,128)S(1)} %get-tuple-element.29), channel_id=1, source_target_pairs={{1,0},{2,1},{3,2},{4,3},{5,4},{6,5},{7,6},{8,7},{9,8},{10,9},{11,1... | collective-permute-start | bytes 1032200 | tf_op jit(solution)/shard_map/ppermute | solution.py:442
